TPU v7x, 256 devices: a whole 4x4x8 slice. The times are simulated.
256 devices in a mesh: seq: 32 (over z, y), head: 8 (over x, core).
Axes of the slice: x: 4, y: 4, z: 8, core: 2. Of those that a mesh axis runs over, the one named last changes fastest.
Arguments:
- query: bfloat16 [32768, 4096], P('seq', 'head'), may hold values from -0.15625 to 0.15625
- key: bfloat16 [32768, 4096], P('seq', 'head'), may hold values from -0.15625 to 0.15625
- value: bfloat16 [32768, 4096], P('seq', 'head'), may hold values from -18 to 18, as said below
- level_coef: float32 [6, 32, 32768], P(None, 'head', 'seq'), may hold values from 0.25 to 2.5
- gain: float32 [4096], P('head'), may hold values from 0.5 to 1.5
- cotangent: bfloat16 [32768, 4096], P('seq', 'head'), may hold values from -0.625 to 0.625
Outputs:
- mixed: bfloat16 [32768, 4096], P('seq', 'head')
- grad_query: bfloat16 [32768, 4096], P('seq', 'head')
- grad_key: bfloat16 [32768, 4096], P('seq', 'head')
- grad_value: bfloat16 [32768, 4096], P('seq', 'head')
- grad_level: float32 [6, 32, 32768], P(None, 'head', 'seq')
- grad_gain: float32 [4096], P('head')
Inputs may be any that keep to these rules, and one draw needn't show every extreme that they name: `value`: real values.
All inputs are finite; a program needn't handle non-finite values.
Results may differ from a plain program's by a relative error of at most 0.0065.
Values sent between devices are 32-bit elements; how exact they have to be, the bound alone decides.
A program may use at most 128 MiB of HBM per device.

v0:
```python
import jax
import jax.numpy as jnp
from jax import lax
from jax.sharding import PartitionSpec as P

HEADS = 32
HEAD_DIM = 128


EPS = 1e-06


def from_partner(block, axis, apart):
    count = lax.axis_size(axis)
    route = []
    for low in range(count):
        high = low | 1 << apart
        if high != low and high < count:
            route += [(low, high), (high, low)]
    return lax.ppermute(block, axis, route)


def sent_to_all(array, axis):
    copies = jnp.broadcast_to(array, (lax.axis_size(axis), *array.shape))
    return lax.all_to_all(copies, axis, split_axis=0, concat_axis=0, tiled=True)


def taken_together(array, axis):
    return sent_to_all(array, axis).sum(axis=0)


def body(query, key, value, level_coef, gain, cotangent):
    f32 = jnp.float32
    bf16 = jnp.bfloat16
    rows = query.shape[0]
    heads_here = level_coef.shape[1]
    width = query.shape[1] // heads_here
    depth = level_coef.shape[0] - 1
    group = lax.axis_index("seq")
    q_three = query.reshape(rows, heads_here, width)
    k_three = key.reshape(rows, heads_here, width)
    v_three = value.reshape(rows, heads_here, width)
    scores = jnp.einsum("the,she->hts", q_three, k_three, preferred_element_type=f32)
    causal = lax.broadcasted_iota(jnp.int32, (rows, rows), 0) >= lax.broadcasted_iota(
        jnp.int32, (rows, rows), 1
    )
    kept = jnp.where(causal[None], scores, 0.0).astype(bf16)
    local = jnp.einsum("hts,she->the", kept, v_three, preferred_element_type=f32)
    states = jnp.einsum("sha,shb->hab", k_three, v_three, preferred_element_type=f32)
    bits = [(group // 2**level % 2).astype(f32) for level in range(depth)]
    block = states
    found = []
    for level in range(depth):
        other = from_partner(block, "seq", level)
        found.append(bits[level] * other)
        block = block + other
    buckets = jnp.stack(found)
    bucket_half = buckets.astype(bf16)
    reads = jnp.einsum("the,lhef->lthf", q_three, bucket_half, preferred_element_type=f32)
    first = level_coef[0].T[:, :, None]
    rest = level_coef[1:].transpose(0, 2, 1)[..., None]
    output = first * local + jnp.sum(rest * reads, axis=0)
    squares = taken_together(jnp.sum(output * output, axis=(1, 2)), "head")
    scale = lax.rsqrt(squares / (HEADS * HEAD_DIM) + EPS)[:, None, None]
    normed = output * scale
    gain_three = gain.reshape(heads_here, width)
    mixed = (normed * gain_three).astype(bf16).reshape(rows, -1)
    cot_three = cotangent.reshape(rows, heads_here, width).astype(f32)
    grad_gain = taken_together(jnp.sum(cot_three * normed, axis=0).reshape(-1), "seq")
    weighted_cot = cot_three * gain_three
    inner = taken_together(jnp.sum(weighted_cot * output, axis=(1, 2)), "head")
    grad_full = (
        weighted_cot - output * (inner[:, None, None] * scale * scale / (HEADS * HEAD_DIM))
    ) * scale
    grad_half = grad_full.astype(bf16)
    grad_float = grad_half.astype(f32)
    grad_first = jnp.sum(grad_float * local, axis=-1)
    grad_rest = jnp.sum(grad_float[None] * reads, axis=-1)
    grad_level = jnp.concatenate([grad_first.T[None], grad_rest.transpose(0, 2, 1)], axis=0)
    weighted = (first * grad_float).astype(bf16)
    value_sum = jnp.einsum("hts,the->she", kept, weighted, preferred_element_type=f32)
    pair = (
        jnp.einsum("the,she->hts", grad_half, v_three, preferred_element_type=f32)
        * level_coef[0][:, :, None]
    )
    pair = jnp.where(causal[None], pair, 0.0).astype(bf16)
    query_sum = jnp.einsum("hts,she->the", pair, k_three, preferred_element_type=f32)
    key_sum = jnp.einsum("hts,the->she", pair, q_three, preferred_element_type=f32)
    scaled = (rest * grad_float[None]).astype(bf16)
    query_sum = query_sum + jnp.einsum(
        "lthf,lhef->the", scaled, bucket_half, preferred_element_type=f32
    )
    grad_buckets = jnp.einsum("the,lthf->lhef", q_three, scaled, preferred_element_type=f32)
    masks = jnp.stack(bits)[:, None, None, None]
    pending = masks * grad_buckets
    carried = jnp.zeros_like(states)
    for level in range(depth):
        other = from_partner(pending, "seq", level)
        carried = carried + (1.0 - bits[level]) * other[0]
        pending = pending[1:] + other[1:]
    grad_states = carried.astype(bf16)
    key_sum = key_sum + jnp.einsum("shb,hab->sha", v_three, grad_states, preferred_element_type=f32)
    value_sum = value_sum + jnp.einsum(
        "sha,hab->shb", k_three, grad_states, preferred_element_type=f32
    )
    grad_query = query_sum.astype(bf16).reshape(rows, -1)
    grad_key = key_sum.astype(bf16).reshape(rows, -1)
    grad_value = value_sum.astype(bf16).reshape(rows, -1)
    return (mixed, grad_query, grad_key, grad_value, grad_level, grad_gain)


def solution(mesh):
    placed = (
        P("seq", "head"),
        P("seq", "head"),
        P("seq", "head"),
        P(None, "head", "seq"),
        P("head"),
        P("seq", "head"),
    )
    return jax.shard_map(
        body,
        mesh=mesh,
        in_specs=placed,
        out_specs=(
            P("seq", "head"),
            P("seq", "head"),
            P("seq", "head"),
            P("seq", "head"),
            P(None, "head", "seq"),
            P("head"),
        ),
        check_vma=False,
    )
```

profile of v0, /device:TPU:6, one launch (start us, length us, event | category | flops | bytes accessed | tf_op | source)
XLA Modules:
  0.0 236.6 jit_solution(10579166406929933592)
XLA Ops:
  7.1 4.6 %collective-permute-done = f32[4,128,128]{2,1,0:T(8,128)S(1)} collective-permute-done((f32[4,128,128]{2,1,0:T(8,128)}, f32[4,128,128]{2,1,0:T(8,128)S(1)}, u32[]{:S(2)}, u32[]{:S(2)}) %collective-permute-start) | collective-permute-done | bytes 262176 | tf_op jit(solution)/shard_map/ppermute | solution.py:20
  12.7 3.3 %collective-permute-start.1 = (f32[4,128,128]{2,1,0:T(8,128)S(1)}, f32[4,128,128]{2,1,0:T(8,128)S(1)}, u32[]{:S(2)}, u32[]{:S(2)}) collective-permute-start(f32[4,128,128]{2,1,0:T(8,128)S(1)} %add.90), channel_id=1, source_target_pairs={{0,16},{16,0},{8,24},{24,8},{32,48},{48,32},{40,56},{56,40},{64,80... | collective-permute-start | bytes 786440 | tf_op jit(solution)/shard_map/ppermute | solution.py:20
  16.0 7.2 %select_convert_fusion.1 = bf16[4,1024,1024]{2,1,0:T(8,128)(2,1)} fusion(bf16[1024,4,128]{0,2,1:T(8,128)(2,1)} %copy.97, pred[1024,1024]{1,0:T(8,128)(4,1)S(1)} %iota_compare_fusion, bf16[1024,512]{1,0:T(8,128)(2,1)S(1)} %copy-done.12), kind=kOutput, calls=%fused_computation.1 | convolution fusion | flops 1082130432 | bytes 11534336 | tf_op jit(solution)/shard_map/the,she->hts/dot_general | solution.py:43
  27.4 3.6 %collective-permute-done.2 = f32[4,128,128]{2,1,0:T(8,128)S(1)} collective-permute-done((f32[4,128,128]{2,1,0:T(8,128)S(1)}, f32[4,128,128]{2,1,0:T(8,128)S(1)}, u32[]{:S(2)}, u32[]{:S(2)}) %collective-permute-start.2) | collective-permute-done | bytes 262176 | tf_op jit(solution)/shard_map/ppermute | solution.py:20
  31.0 3.4 %collective-permute-start.3 = (f32[4,128,128]{2,1,0:T(8,128)S(1)}, f32[4,128,128]{2,1,0:T(8,128)S(1)}, u32[]{:S(2)}, u32[]{:S(2)}) collective-permute-start(f32[4,128,128]{2,1,0:T(8,128)S(1)} %add.94), channel_id=1, source_target_pairs={{0,64},{64,0},{8,72},{72,8},{16,80},{80,16},{24,88},{88,24},{32,96... | collective-permute-start | bytes 786440 | tf_op jit(solution)/shard_map/ppermute | solution.py:20
  35.4 9.0 %collective-permute-done.3 = f32[4,128,128]{2,1,0:T(8,128)S(1)} collective-permute-done((f32[4,128,128]{2,1,0:T(8,128)S(1)}, f32[4,128,128]{2,1,0:T(8,128)S(1)}, u32[]{:S(2)}, u32[]{:S(2)}) %collective-permute-start.3) | collective-permute-done | bytes 262176 | tf_op jit(solution)/shard_map/ppermute | solution.py:20
  44.4 6.3 %collective-permute-start.4 = (f32[4,128,128]{2,1,0:T(8,128)S(1)}, f32[4,128,128]{2,1,0:T(8,128)S(1)}, u32[]{:S(2)}, u32[]{:S(2)}) collective-permute-start(f32[4,128,128]{2,1,0:T(8,128)S(1)} %add.96), channel_id=1, source_target_pairs={{0,128},{128,0},{8,136},{136,8},{16,144},{144,16},{24,152},{152,24... | collective-permute-start | bytes 786440 | tf_op jit(solution)/shard_map/ppermute | solution.py:20
  50.8 11.6 %collective-permute-done.4 = f32[4,128,128]{2,1,0:T(8,128)S(1)} collective-permute-done((f32[4,128,128]{2,1,0:T(8,128)S(1)}, f32[4,128,128]{2,1,0:T(8,128)S(1)}, u32[]{:S(2)}, u32[]{:S(2)}) %collective-permute-start.4) | collective-permute-done | bytes 262176 | tf_op jit(solution)/shard_map/ppermute | solution.py:20
  62.5 7.6 %fusion = (f32[1024,4,128]{0,2,1:T(8,128)}, f32[4,5,128,1024]{3,2,1,0:T(8,128)}) fusion(f32[5,1024,4]{1,0,2:T(8,128)S(1)} %copy.85, bf16[1024,4,128,1]{2,1,0,3:T(4,128)(2,1)S(1)} %bitcast.136, bf16[5,4,128,128]{3,2,1,0:T(8,128)(2,1)S(1)} %fusion.46), kind=kOutput, calls=%fused_computation.4 | convolution fusion | flops 675807232 | bytes 14368768 | tf_op jit(solution)/shard_map/the,lhef->lthf/dot_general | solution.py:59
  70.1 6.6 %multiply_reduce_fusion.2 = (f32[1024]{0:T(1024)S(1)}, f32[1024,4,128]{0,2,1:T(8,128)}, f32[4,1024,128]{1,2,0:T(8,128)}) fusion(f32[1024,4,128]{0,2,1:T(8,128)} %get-tuple-element.41, f32[1024,4]{0,1:T(4,128)S(1)} %get-tuple-element.40, bf16[4,1024,1024]{2,1,0:T(8,128)(2,1)S(1)} %bitcast.132, bf16[1024,512]{1,0:T(8,128)(2,1)S(1)} %copy-done), kind=kOutput, calls=%fused_computation.24 | convolution fusion | flops 1075837952 | bytes 15749120 | tf_op jit(solution)/shard_map/hts,she->the/dot_general | solution.py:48
  77.3 4.8 %all-to-all-start = ((f32[8,1,1024]{2,1,0:T(1,128)}), f32[8,1,1024]{2,1,0:T(1,128)S(1)}, u32[]{:S(2)}, u32[]{:S(2)}) async-start(f32[8,1,1024]{2,1,0:T(1,128)} %broadcast_in_dim.43), calls=%async_computation | async-start | bytes 65536 | tf_op jit(solution)/shard_map/all_to_all | solution.py:25
  88.3 5.3 %all-to-all-start.1 = ((f32[8,1,1024]{2,1,0:T(1,128)}), f32[8,1,1024]{2,1,0:T(1,128)S(1)}, u32[]{:S(2)}, u32[]{:S(2)}) async-start(f32[8,1,1024]{2,1,0:T(1,128)} %broadcast_in_dim.44), calls=%async_computation.1 | async-start | bytes 65536 | tf_op jit(solution)/shard_map/all_to_all | solution.py:25
  93.8 3.3 %all-to-all-done.1 = f32[8,1,1024]{2,1,0:T(1,128)S(1)} async-done(((f32[8,1,1024]{2,1,0:T(1,128)}), f32[8,1,1024]{2,1,0:T(1,128)S(1)}, u32[]{:S(2)}, u32[]{:S(2)}) %all-to-all-start.1) | async-done | bytes 32800 | tf_op jit(solution)/shard_map/all_to_all | solution.py:25
  97.1 3.9 %fusion.7 = (f32[1024,4]{0,1:T(4,128)S(1)}, bf16[1024,4,128]{0,2,1:T(8,128)(2,1)S(1)}, bf16[1024,4,128]{0,2,1:T(8,128)(2,1)}) fusion(f32[4,1024,128]{1,2,0:T(8,128)} %get-tuple-element.43, f32[1024]{0:T(1024)S(1)} %add_rsqrt_fusion, f32[1024,4,128]{0,2,1:T(8,128)} %get-tuple-element.35, f32[1024]{0:T(1024)S(1)} %fusion.49, f32[4,128]{1,0:T(4,128)S(1)} %bitcast.148, ...), kind=kLoop, calls=%fused_computation.17 | loop fusion | flops 5763072 | bytes 8415232 | tf_op jit(solution)/shard_map/reduce_sum | solution.py:77
  102.6 2.6 %fusion.10 = f32[5,4,128,128]{2,3,0,1:T(8,128)} fusion(bf16[1024,4,128,1]{2,1,0,3:T(4,128)(2,1)S(1)} %bitcast.137, f32[5]{0:T(128)S(1)} %stack.53, f32[1024,4,128]{0,2,1:T(8,128)S(1)} %convert_element_type.69, f32[5,1024,4]{1,0,2:T(8,128)S(1)} %copy.85), kind=kOutput, calls=%fused_computation.26 | convolution fusion | flops 676659200 | bytes 4538388 | tf_op jit(solution)/shard_map/the,lthf->lhef/dot_general | solution.py:93
  106.6 5.9 %all-to-all-start.2 = ((f32[32,1,512]{2,1,0:T(1,128)}), f32[32,1,512]{2,1,0:T(1,128)S(1)}, u32[]{:S(2)}, u32[]{:S(2)}) async-start(f32[32,1,512]{2,1,0:T(1,128)} %broadcast_in_dim.47), calls=%async_computation.2 | async-start | bytes 131072 | tf_op jit(solution)/shard_map/all_to_all | solution.py:25
  112.4 24.2 %collective-permute-done.5 = f32[5,4,128,128]{2,3,0,1:T(8,128)} collective-permute-done((f32[5,4,128,128]{2,3,0,1:T(8,128)}, f32[5,4,128,128]{2,3,0,1:T(8,128)}, u32[]{:S(2)}, u32[]{:S(2)}) %collective-permute-start.5) | collective-permute-done | bytes 1310752 | tf_op jit(solution)/shard_map/ppermute | solution.py:20
  136.7 2.6 %slice_add_fusion = f32[4,4,128,128]{2,3,0,1:T(8,128)} fusion(f32[5,4,128,128]{2,3,0,1:T(8,128)} %collective-permute-done.5, f32[5,4,128,128]{2,3,0,1:T(8,128)} %fusion.10), kind=kLoop, calls=%fused_computation.36 | loop fusion | flops 262144 | bytes 3145728 | tf_op jit(solution)/shard_map/add | solution.py:100
  139.8 4.9 %select_convert_fusion = bf16[4,1024,1024]{2,1,0:T(8,128)(2,1)S(1)} fusion(bf16[1024,4,128]{0,2,1:T(8,128)(2,1)S(1)} %copy-done.5, f32[4,1024]{1,0:T(4,128)S(1)} %copy-done.21, pred[1024,1024]{1,0:T(8,128)(4,1)} %copy-done.18, bf16[1024,512]{1,0:T(8,128)(2,1)S(1)} %copy-done), kind=kOutput, calls=%fused_computation | convolution fusion | flops 1086324736 | bytes 11550720 | tf_op jit(solution)/shard_map/the,she->hts/dot_general | solution.py:83
  144.8 6.2 %fusion.51 = f32[4,1024,128]{1,2,0:T(8,128)} fusion(bf16[4,1024,1024]{2,1,0:T(8,128)(2,1)S(1)} %select_convert_fusion, bf16[1024,4,128]{0,2,1:T(8,128)(2,1)} %bitcast.142), kind=kOutput, calls=%fused_computation.85 | convolution fusion | flops 1073741824 | bytes 11534336 | tf_op jit(solution)/shard_map/hts,she->the/dot_general | solution.py:87
  151.0 14.0 %collective-permute-done.6 = f32[4,4,128,128]{2,3,0,1:T(8,128)} collective-permute-done((f32[4,4,128,128]{2,3,0,1:T(8,128)}, f32[4,4,128,128]{2,3,0,1:T(8,128)}, u32[]{:S(2)}, u32[]{:S(2)}) %collective-permute-start.6) | collective-permute-done | bytes 1048608 | tf_op jit(solution)/shard_map/ppermute | solution.py:20
  165.0 2.3 slice_add_fusion.1
  167.4 2.6 %fusion.11 = f32[4,128,1024]{2,1,0:T(8,128)} fusion(bf16[4,1024,1024]{2,1,0:T(8,128)(2,1)S(1)} %bitcast.134, bf16[1024,4,128]{0,2,1:T(8,128)(2,1)S(1)} %copy-done.5, f32[1024,4]{0,1:T(4,128)S(1)} %get-tuple-element.40), kind=kOutput, calls=%fused_computation.27 | convolution fusion | flops 1075314688 | bytes 11550720 | tf_op jit(solution)/shard_map/hts,the->she/dot_general | solution.py:81
  170.0 6.8 %fusion.1 = (f32[5,1024,4]{1,0,2:T(8,128)S(1)}, bf16[5,1024,4,128]{1,3,0,2:T(8,128)(2,1)S(1)}) fusion(f32[4,5,128,1024]{3,2,1,0:T(8,128)} %get-tuple-element.42, f32[1024,4,128]{0,2,1:T(8,128)} %copy-done.6, f32[5,1024,4]{1,0,2:T(8,128)S(1)} %copy.85), kind=kLoop, calls=%fused_computation.5 | loop fusion | flops 10465280 | bytes 17989632 | tf_op jit(solution)/shard_map/reduce_sum | solution.py:78
  176.8 8.3 %collective-permute-done.7 = f32[3,4,128,128]{2,3,0,1:T(8,128)} collective-permute-done((f32[3,4,128,128]{2,3,0,1:T(8,128)}, f32[3,4,128,128]{2,3,0,1:T(8,128)}, u32[]{:S(2)}, u32[]{:S(2)}) %collective-permute-start.7) | collective-permute-done | bytes 786464 | tf_op jit(solution)/shard_map/ppermute | solution.py:20
  188.5 6.0 %fusion.52 = f32[4,1024,128]{1,2,0:T(8,128)} fusion(bf16[1024,4,128]{0,2,1:T(8,128)(2,1)S(1)} %copy-done.14, bf16[4,1024,1024]{2,1,0:T(8,128)(2,1)} %copy-done.1), kind=kOutput, calls=%fused_computation.86 | convolution fusion | flops 1073741824 | bytes 11534336 | tf_op jit(solution)/shard_map/hts,the->she/dot_general | solution.py:88
  194.5 14.9 %collective-permute-done.8 = f32[2,4,128,128]{2,3,0,1:T(8,128)S(1)} collective-permute-done((f32[2,4,128,128]{2,3,0,1:T(8,128)S(1)}, f32[2,4,128,128]{2,3,0,1:T(8,128)S(1)}, u32[]{:S(2)}, u32[]{:S(2)}) %collective-permute-start.8) | collective-permute-done | bytes 524320 | tf_op jit(solution)/shard_map/ppermute | solution.py:20
  210.2 3.1 %collective-permute-start.9 = (f32[1,4,128,128]{2,3,0,1:T(8,128)}, f32[1,4,128,128]{2,3,0,1:T(8,128)}, u32[]{:S(2)}, u32[]{:S(2)}) collective-permute-start(f32[1,4,128,128]{2,3,0,1:T(8,128)} %slice_add_fusion.3), channel_id=1, source_target_pairs={{0,128},{128,0},{8,136},{136,8},{16,144},{144,16},{24,152},{152,24... | collective-permute-start | bytes 786440 | tf_op jit(solution)/shard_map/ppermute | solution.py:20
  215.4 2.3 copy.103
  218.4 2.3 copy.104
  221.3 6.2 %collective-permute-done.9 = f32[1,4,128,128]{2,3,0,1:T(8,128)} collective-permute-done((f32[1,4,128,128]{2,3,0,1:T(8,128)}, f32[1,4,128,128]{2,3,0,1:T(8,128)}, u32[]{:S(2)}, u32[]{:S(2)}) %collective-permute-start.9) | collective-permute-done | bytes 262176 | tf_op jit(solution)/shard_map/ppermute | solution.py:20
  230.4 2.4 %copy.106 = bf16[1024,512]{1,0:T(8,128)(2,1)} copy(bf16[1024,512]{0,1:T(8,128)(2,1)} %bitcast.140) | data formatting | bytes 2097152
  (104 shorter events, 37.3 us)
Async XLA Ops:
  3.5 8.3 %collective-permute-start = (f32[4,128,128]{2,1,0:T(8,128)}, f32[4,128,128]{2,1,0:T(8,128)S(1)}, u32[]{:S(2)}, u32[]{:S(2)}) collective-permute-start(f32[4,128,128]{2,1,0:T(8,128)} %fusion.16), channel_id=1, source_target_pairs={{0,8},{8,0},{16,24},{24,16},{32,40},{40,32},{48,56},{56,48},{64,72... | collective-permute-start | bytes 786440 | tf_op jit(solution)/shard_map/ppermute | solution.py:20
  5.3 57.2 %copy-start.2 = (bf16[1024,4,128]{2,1,0:T(4,128)(2,1)}, bf16[1024,4,128]{2,1,0:T(4,128)(2,1)S(1)}, u32[]{:S(2)}) copy-start(bf16[1024,4,128]{2,1,0:T(4,128)(2,1)S(1)} %reshape.93) | copy-start | bytes 3145732
  5.3 10.7 %copy-start.12 = (bf16[1024,512]{1,0:T(8,128)(2,1)S(1)}, bf16[1024,512]{1,0:T(8,128)(2,1)}, u32[]{:S(2)}) copy-start(bf16[1024,512]{1,0:T(8,128)(2,1)} %param.7) | copy-start | bytes 3145732
  7.1 16.1 %copy-start.18 = (pred[1024,1024]{1,0:T(8,128)(4,1)}, pred[1024,1024]{1,0:T(8,128)(4,1)S(1)}, u32[]{:S(2)}) copy-start(pred[1024,1024]{1,0:T(8,128)(4,1)S(1)} %iota_compare_fusion) | copy-start | bytes 3145732
  12.7 13.2 %copy-start.20 = (f32[6,4,1024]{2,1,0:T(4,128)S(1)}, f32[6,4,1024]{2,1,0:T(4,128)}, u32[]{:S(2)}) copy-start(f32[6,4,1024]{2,1,0:T(4,128)} %param.9) | copy-start | bytes 294916
  12.7 10.5 %collective-permute-start.1 = (f32[4,128,128]{2,1,0:T(8,128)S(1)}, f32[4,128,128]{2,1,0:T(8,128)S(1)}, u32[]{:S(2)}, u32[]{:S(2)}) collective-permute-start(f32[4,128,128]{2,1,0:T(8,128)S(1)} %add.90), channel_id=1, source_target_pairs={{0,16},{16,0},{8,24},{24,8},{32,48},{48,32},{40,56},{56,40},{64,80... | collective-permute-start | bytes 786440 | tf_op jit(solution)/shard_map/ppermute | solution.py:20
  23.9 7.1 %collective-permute-start.2 = (f32[4,128,128]{2,1,0:T(8,128)S(1)}, f32[4,128,128]{2,1,0:T(8,128)S(1)}, u32[]{:S(2)}, u32[]{:S(2)}) collective-permute-start(f32[4,128,128]{2,1,0:T(8,128)S(1)} %add.92), channel_id=1, source_target_pairs={{0,32},{32,0},{8,40},{40,8},{16,48},{48,16},{24,56},{56,24},{64,96... | collective-permute-start | bytes 786440 | tf_op jit(solution)/shard_map/ppermute | solution.py:20
  31.0 13.4 %collective-permute-start.3 = (f32[4,128,128]{2,1,0:T(8,128)S(1)}, f32[4,128,128]{2,1,0:T(8,128)S(1)}, u32[]{:S(2)}, u32[]{:S(2)}) collective-permute-start(f32[4,128,128]{2,1,0:T(8,128)S(1)} %add.94), channel_id=1, source_target_pairs={{0,64},{64,0},{8,72},{72,8},{16,80},{80,16},{24,88},{88,24},{32,96... | collective-permute-start | bytes 786440 | tf_op jit(solution)/shard_map/ppermute | solution.py:20
  44.4 18.0 %collective-permute-start.4 = (f32[4,128,128]{2,1,0:T(8,128)S(1)}, f32[4,128,128]{2,1,0:T(8,128)S(1)}, u32[]{:S(2)}, u32[]{:S(2)}) collective-permute-start(f32[4,128,128]{2,1,0:T(8,128)S(1)} %add.96), channel_id=1, source_target_pairs={{0,128},{128,0},{8,136},{136,8},{16,144},{144,16},{24,152},{152,24... | collective-permute-start | bytes 786440 | tf_op jit(solution)/shard_map/ppermute | solution.py:20
  62.5 7.6 %copy-start.10 = (bf16[5,4,128,128]{3,2,1,0:T(8,128)(2,1)}, bf16[5,4,128,128]{3,2,1,0:T(8,128)(2,1)S(1)}, u32[]{:S(2)}) copy-start(bf16[5,4,128,128]{3,2,1,0:T(8,128)(2,1)S(1)} %fusion.46) | copy-start | bytes 1966084
  62.5 7.6 %slice-start = ((s8[8388608]{0:T(1024)(128)(4,1)}), s8[4194304]{0:T(1024)(128)(4,1)S(1)}, s32[]{:S(2)}) async-start(s8[8388608]{0:T(1024)(128)(4,1)} %bitcast.131), calls=%async_computation.3 | async-start | bytes 8388608
  62.5 7.6 %slice-start.1 = ((s8[8388608]{0:T(1024)(128)(4,1)}), s8[4194304]{0:T(1024)(128)(4,1)S(1)}, s32[]{:S(2)}) async-start(s8[8388608]{0:T(1024)(128)(4,1)} %bitcast.131), calls=%async_computation.4 | async-start | bytes 8388608
  76.7 8.8 %copy-start.22 = (f32[512]{0:T(512)S(1)}, f32[512]{0:T(512)}, u32[]{:S(2)}) copy-start(f32[512]{0:T(512)} %param.10) | copy-start | bytes 6148
  77.3 8.2 %all-to-all-start = ((f32[8,1,1024]{2,1,0:T(1,128)}), f32[8,1,1024]{2,1,0:T(1,128)S(1)}, u32[]{:S(2)}, u32[]{:S(2)}) async-start(f32[8,1,1024]{2,1,0:T(1,128)} %broadcast_in_dim.43), calls=%async_computation | async-start | bytes 65536 | tf_op jit(solution)/shard_map/all_to_all | solution.py:25
  88.3 8.7 %all-to-all-start.1 = ((f32[8,1,1024]{2,1,0:T(1,128)}), f32[8,1,1024]{2,1,0:T(1,128)S(1)}, u32[]{:S(2)}, u32[]{:S(2)}) async-start(f32[8,1,1024]{2,1,0:T(1,128)} %broadcast_in_dim.44), calls=%async_computation.1 | async-start | bytes 65536 | tf_op jit(solution)/shard_map/all_to_all | solution.py:25
  105.2 34.6 %copy-start.21 = (f32[4,1024]{1,0:T(4,128)S(1)}, f32[4,1024]{1,0:T(4,128)}, u32[]{:S(2)}) copy-start(f32[4,1024]{1,0:T(4,128)} %get-tuple-element.39) | copy-start | bytes 49156
  105.2 31.4 %collective-permute-start.5 = (f32[5,4,128,128]{2,3,0,1:T(8,128)}, f32[5,4,128,128]{2,3,0,1:T(8,128)}, u32[]{:S(2)}, u32[]{:S(2)}) collective-permute-start(f32[5,4,128,128]{2,3,0,1:T(8,128)} %fusion.10), channel_id=1, source_target_pairs={{0,8},{8,0},{16,24},{24,16},{32,40},{40,32},{48,56},{56,48},{64,72... | collective-permute-start | bytes 3932168 | tf_op jit(solution)/shard_map/ppermute | solution.py:20
  105.9 33.9 %copy-start.5 = (bf16[1024,4,128]{0,2,1:T(8,128)(2,1)S(1)}, bf16[1024,4,128]{0,2,1:T(8,128)(2,1)}, u32[]{:S(2)}) copy-start(bf16[1024,4,128]{0,2,1:T(8,128)(2,1)} %copy-done.4) | copy-start | bytes 3145732
  106.6 114.1 %all-to-all-start.2 = ((f32[32,1,512]{2,1,0:T(1,128)}), f32[32,1,512]{2,1,0:T(1,128)S(1)}, u32[]{:S(2)}, u32[]{:S(2)}) async-start(f32[32,1,512]{2,1,0:T(1,128)} %broadcast_in_dim.47), calls=%async_computation.2 | async-start | bytes 131072 | tf_op jit(solution)/shard_map/all_to_all | solution.py:25
  139.3 25.7 %collective-permute-start.6 = (f32[4,4,128,128]{2,3,0,1:T(8,128)}, f32[4,4,128,128]{2,3,0,1:T(8,128)}, u32[]{:S(2)}, u32[]{:S(2)}) collective-permute-start(f32[4,4,128,128]{2,3,0,1:T(8,128)} %slice_add_fusion), channel_id=1, source_target_pairs={{0,16},{16,0},{8,24},{24,8},{32,48},{48,32},{40,56},{56,40},{64,80... | collective-permute-start | bytes 3145736 | tf_op jit(solution)/shard_map/ppermute | solution.py:20
  139.8 27.6 %slice-start.2 = ((s8[8388608]{0:T(1024)(128)(4,1)}), s8[4194304]{0:T(1024)(128)(4,1)S(1)}, s32[]{:S(2)}) async-start(s8[8388608]{0:T(1024)(128)(4,1)} %bitcast.133), calls=%async_computation.5 | async-start | bytes 8388608
  139.8 27.5 %slice-start.3 = ((s8[8388608]{0:T(1024)(128)(4,1)}), s8[4194304]{0:T(1024)(128)(4,1)S(1)}, s32[]{:S(2)}) async-start(s8[8388608]{0:T(1024)(128)(4,1)} %bitcast.133), calls=%async_computation.6 | async-start | bytes 8388608
  144.8 6.2 %copy-start.1 = (bf16[4,1024,1024]{2,1,0:T(8,128)(2,1)}, bf16[4,1024,1024]{2,1,0:T(8,128)(2,1)S(1)}, u32[]{:S(2)}) copy-start(bf16[4,1024,1024]{2,1,0:T(8,128)(2,1)S(1)} %select_convert_fusion) | copy-start | bytes 25165828
  167.4 17.7 %collective-permute-start.7 = (f32[3,4,128,128]{2,3,0,1:T(8,128)}, f32[3,4,128,128]{2,3,0,1:T(8,128)}, u32[]{:S(2)}, u32[]{:S(2)}) collective-permute-start(f32[3,4,128,128]{2,3,0,1:T(8,128)} %slice_add_fusion.1), channel_id=1, source_target_pairs={{0,32},{32,0},{8,40},{40,8},{16,48},{48,16},{24,56},{56,24},{64,96... | collective-permute-start | bytes 2359304 | tf_op jit(solution)/shard_map/ppermute | solution.py:20
  176.8 11.7 %copy-start.14 = (bf16[1024,4,128]{0,2,1:T(8,128)(2,1)S(1)}, bf16[1024,4,128]{0,2,1:T(8,128)(2,1)}, u32[]{:S(2)}) copy-start(bf16[1024,4,128]{0,2,1:T(8,128)(2,1)} %copy.97) | copy-start | bytes 3145732
  186.3 27.0 %copy-start.7 = (f32[4,1024,128]{1,2,0:T(8,128)S(1)}, f32[4,1024,128]{1,2,0:T(8,128)}, u32[]{:S(2)}) copy-start(f32[4,1024,128]{1,2,0:T(8,128)} %fusion.51) | copy-start | bytes 6291460
  186.3 27.0 %copy-start.11 = (bf16[5,4,128,128]{3,2,1,0:T(8,128)(2,1)S(1)}, bf16[5,4,128,128]{3,2,1,0:T(8,128)(2,1)}, u32[]{:S(2)}) copy-start(bf16[5,4,128,128]{3,2,1,0:T(8,128)(2,1)} %copy-done.10) | copy-start | bytes 1966084
  186.3 23.1 %collective-permute-start.8 = (f32[2,4,128,128]{2,3,0,1:T(8,128)S(1)}, f32[2,4,128,128]{2,3,0,1:T(8,128)S(1)}, u32[]{:S(2)}, u32[]{:S(2)}) collective-permute-start(f32[2,4,128,128]{2,3,0,1:T(8,128)S(1)} %slice_add_fusion.2), channel_id=1, source_target_pairs={{0,64},{64,0},{8,72},{72,8},{16,80},{80,16},{24,88},{88,24},{32,96... | collective-permute-start | bytes 1572872 | tf_op jit(solution)/shard_map/ppermute | solution.py:20
  209.4 6.0 %copy-start.19 = (f32[2,4,128,128]{2,3,0,1:T(8,128)}, f32[2,4,128,128]{2,3,0,1:T(8,128)S(1)}, u32[]{:S(2)}) copy-start(f32[2,4,128,128]{2,3,0,1:T(8,128)S(1)} %collective-permute-done.8) | copy-start | bytes 1572868
  210.2 17.4 %collective-permute-start.9 = (f32[1,4,128,128]{2,3,0,1:T(8,128)}, f32[1,4,128,128]{2,3,0,1:T(8,128)}, u32[]{:S(2)}, u32[]{:S(2)}) collective-permute-start(f32[1,4,128,128]{2,3,0,1:T(8,128)} %slice_add_fusion.3), channel_id=1, source_target_pairs={{0,128},{128,0},{8,136},{136,8},{16,144},{144,16},{24,152},{152,24... | collective-permute-start | bytes 786440 | tf_op jit(solution)/shard_map/ppermute | solution.py:20
  217.7 11.2 %copy-start.8 = (f32[4,128,1024]{2,1,0:T(8,128)S(1)}, f32[4,128,1024]{2,1,0:T(8,128)}, u32[]{:S(2)}) copy-start(f32[4,128,1024]{2,1,0:T(8,128)} %fusion.11) | copy-start | bytes 6291460
  221.3 7.6 %copy-start.13 = (bf16[1024,512]{1,0:T(8,128)(2,1)S(1)}, bf16[1024,512]{1,0:T(8,128)(2,1)}, u32[]{:S(2)}) copy-start(bf16[1024,512]{1,0:T(8,128)(2,1)} %param.7) | copy-start | bytes 3145732
  (8 other events, 18.8 us)
where the time goes:
time: 240 us; the launch traced here: 237 us
  waiting for transfers between devices  102 us (42%)
  matrix products  50 us (21%)
  starting transfers between devices  38.9 us (16%)
  other arithmetic  24.7 us (10%)
  local copies, waits for them, and re-layouts  20.3 us (8%)
    ppermute x10, waiting for transfers between devices, from_partner(): return lax.ppermute(block, axis, route)  96.4 us
    ppermute x10, starting transfers between devices, from_partner(): return lax.ppermute(block, axis, route)  22.9 us
    all_to_all x3, starting transfers between devices, sent_to_all(): return lax.all_to_all(copies, axis, split_axis=0, concat_axis=0, tiled=True)  16 us
    unnamed x59, local copies, waits for them, and re-layouts  12.1 us
    dot_general x1, matrix products, body(): jnp.einsum('the,lhef->lthf', q_three, bucket_half, preferred_element_type...  7.59 us
    dot_general x1, matrix products, body(): jnp.einsum('the,she->hts', q_three, k_three, preferred_element_type=f32)  7.23 us
    add x4, other arithmetic, body(): pending = pending[1:] + other[1:]  7.02 us
    reduce_sum x1, other arithmetic, body(): grad_rest = jnp.sum(grad_float[None] * reads, axis=-1)  6.75 us
  transfers between devices with their start and end apart: 13, of which 11 were waited for; matrix products, arithmetic and copies ran while one was open for 23% of the time, Pallas kernels for 0%

commit v1 on v0

v1 whole, which is shorter than its diff:
```python
import jax
import jax.numpy as jnp
from jax import lax
from jax.experimental import pallas as pl
from jax.experimental.pallas import tpu as pltpu
from jax.sharding import PartitionSpec as P

EPS = 1e-06
F32 = jnp.float32
BF16 = jnp.bfloat16
MESH = pl.DeviceIdType.MESH

NY = 4
NZ = 8
NH = 8
HL = 4
D = 128
T = 1024
C = 256
NC = T // C
SUB = D // NZ


def dot_nn(a, b):
    return lax.dot_general(a, b, (((1,), (0,)), ((), ())), preferred_element_type=F32)


def dot_nt(a, b):
    return lax.dot_general(a, b, (((1,), (1,)), ((), ())), preferred_element_type=F32)


def dot_tn(a, b):
    return lax.dot_general(a, b, (((0,), (0,)), ((), ())), preferred_element_type=F32)


def head_lanes(h):
    return slice(h * D, (h + 1) * D)


def chunk_rows(c, size=C):
    return pl.ds(pl.multiple_of(c * size, size), size)


def when(cond, fn):
    if cond is True:
        fn()
    elif cond is not False:
        pl.when(cond)(fn)


SCRATCH = dict(
    q=pltpu.VMEM((T, HL * D), BF16),
    k=pltpu.VMEM((T, HL * D), BF16),
    v=pltpu.VMEM((T, HL * D), BF16),
    cot=pltpu.VMEM((T, HL * D), BF16),
    lam=pltpu.VMEM((6, HL, T), F32),
    gain=pltpu.VMEM((1, HL * D), F32),
    mixed=pltpu.VMEM((T, HL * D), BF16),
    gq=pltpu.VMEM((T, HL * D), BF16),
    gk=pltpu.VMEM((T, HL * D), BF16),
    gv=pltpu.VMEM((T, HL * D), BF16),
    gl=pltpu.VMEM((6, HL, T), F32),
    lam_rows=pltpu.VMEM((D, T), F32),
    lam_cols=pltpu.VMEM((T, D), F32),
    lam_wide=pltpu.VMEM((6, T, HL * D), F32),
    prefix=pltpu.VMEM((HL * NC, D, D), BF16),
    local=pltpu.VMEM((T, HL * D), F32),
    reads=pltpu.VMEM((HL, T, 5 * D), F32),
    out=pltpu.VMEM((T, HL * D), F32),
    kept_t=pltpu.VMEM((HL * NC, C, C), BF16),
    q_t=pltpu.VMEM((HL, D, T), BF16),
    bcat=pltpu.VMEM((HL, D, 5 * D), BF16),
    fcat=pltpu.VMEM((HL, T, 5 * D), BF16),
    e=pltpu.VMEM((T, HL * D), BF16),
    do=pltpu.VMEM((T, HL * D), BF16),
    ds=pltpu.VMEM((HL * NC, D, D), F32),
    stat_cols=pltpu.VMEM((T, D), F32),
    h_own=pltpu.VMEM((HL, D, D), F32),
    h_y=pltpu.VMEM((NY, D, D), F32),
    t_own=pltpu.VMEM((D, D), F32),
    a_own=pltpu.VMEM((D, D), F32),
    t_z=pltpu.VMEM((NZ, SUB, D), F32),
    pair_z=pltpu.VMEM((2, SUB, D), F32),
    quad_z=pltpu.VMEM((SUB, D), F32),
    b_own=pltpu.VMEM((3, D, D), F32),
    b_all=pltpu.VMEM((5, HL, D, D), F32),
    stat_own=pltpu.VMEM((8, T), F32),
    stat_all=pltpu.VMEM((NH, 8, T), F32),
    db=pltpu.VMEM((5, HL, D, D), F32),
    db_y=pltpu.VMEM((5, NY, D, D), F32),
    u_own=pltpu.VMEM((3, D, D), F32),
    u_z=pltpu.VMEM((3, NZ, SUB, D), F32),
    g_z=pltpu.VMEM((NZ, SUB, D), F32),
    g_own=pltpu.VMEM((D, D), F32),
    dh_own=pltpu.VMEM((NY, D, D), F32),
    dh=pltpu.VMEM((HL, D, D), F32),
    gg_own=pltpu.VMEM((8, HL * D), F32),
    gg_y=pltpu.VMEM((NY, 8, HL * D), F32),
    gg_mid=pltpu.VMEM((8, HL * D), F32),
    gg_z=pltpu.VMEM((NZ, 8, HL * D), F32),
    gg=pltpu.VMEM((1, HL * D), F32),
    sem_in=pltpu.SemaphoreType.DMA((6,)),
    sem_out=pltpu.SemaphoreType.DMA((6,)),
    s_hy=pltpu.SemaphoreType.DMA((NY,)),
    r_hy=pltpu.SemaphoreType.DMA((NY,)),
    s_by=pltpu.SemaphoreType.DMA((2, NY)),
    r_by=pltpu.SemaphoreType.DMA((2, NY)),
    s_tz=pltpu.SemaphoreType.DMA((NZ,)),
    r_tz=pltpu.SemaphoreType.DMA((NZ,)),
    s_bz=pltpu.SemaphoreType.DMA((3, NZ)),
    r_bz=pltpu.SemaphoreType.DMA((3, NZ)),
    s_ba=pltpu.SemaphoreType.DMA((3, NY)),
    r_ba=pltpu.SemaphoreType.DMA((3, NY)),
    s_st=pltpu.SemaphoreType.DMA((NH,)),
    r_st=pltpu.SemaphoreType.DMA((NH,)),
    s_db=pltpu.SemaphoreType.DMA((5, NY)),
    r_db=pltpu.SemaphoreType.DMA((5, NY)),
    s_uz=pltpu.SemaphoreType.DMA((3, NZ)),
    r_uz=pltpu.SemaphoreType.DMA((3, NZ)),
    s_gz=pltpu.SemaphoreType.DMA((NZ,)),
    r_gz=pltpu.SemaphoreType.DMA((NZ,)),
    s_dh=pltpu.SemaphoreType.DMA((NY,)),
    r_dh=pltpu.SemaphoreType.DMA((NY,)),
    s_ggy=pltpu.SemaphoreType.DMA((NY,)),
    r_ggy=pltpu.SemaphoreType.DMA((NY,)),
    s_ggz=pltpu.SemaphoreType.DMA((NZ,)),
    r_ggz=pltpu.SemaphoreType.DMA((NZ,)),
)


class Refs:
    def __init__(self, refs):
        for name, ref in zip(SCRATCH, refs, strict=True):
            setattr(self, name, ref)


def sub_rows(z):
    return pl.ds(pl.multiple_of(z * SUB, SUB), SUB)


def kernel(q_h, k_h, v_h, lam_h, gain_h, cot_h, mixed_h, gq_h, gk_h, gv_h, gl_h, gg_h, *refs):
    r = Refs(refs)
    seq = lax.axis_index("seq")
    head = lax.axis_index("head")
    y = lax.rem(seq, NY)
    z = seq // NY
    zbit = [lax.rem(z // 2**b, 2) == 1 for b in range(3)]
    y_odd = lax.rem(y, 2) == 1
    y_high = y >= 2

    at_y = lambda other: (z * NY + other, head)
    at_z = lambda other: (other * NY + y, head)
    at_head = lambda other: (seq, other)

    sent = []

    def send(cond, src, dst, s_sem, r_sem, device):
        def make():
            return pltpu.make_async_remote_copy(
                src_ref=src,
                dst_ref=dst,
                send_sem=s_sem,
                recv_sem=r_sem,
                device_id=device,
                device_id_type=MESH,
            )

        when(cond, lambda: make().start())
        sent.append((cond, make))

    def receive(cond, dst, s_sem, r_sem, device):
        def wait():
            pltpu.make_async_remote_copy(
                src_ref=dst,
                dst_ref=dst,
                send_sem=s_sem,
                recv_sem=r_sem,
                device_id=device,
                device_id_type=MESH,
            ).wait_recv()

        when(cond, wait)

    ins = [
        pltpu.make_async_copy(src, dst, r.sem_in.at[i])
        for i, (src, dst) in enumerate(
            [(k_h, r.k), (v_h, r.v), (q_h, r.q), (lam_h, r.lam), (cot_h, r.cot), (gain_h, r.gain)]
        )
    ]
    for copy in ins:
        copy.start()

    barrier = pltpu.get_barrier_semaphore()

    def greet(cond, device):
        when(
            cond,
            lambda: pl.semaphore_signal(barrier, inc=1, device_id=device, device_id_type=MESH),
        )

    for other in range(NY):
        greet(y != other, at_y(other))
    for other in range(NZ):
        greet(z != other, at_z(other))
    for other in range(NH):
        greet(head != other, at_head(other))

    ins[0].wait()
    ins[1].wait()
    for h in range(HL):
        acc = jnp.zeros((D, D), F32)
        for c in range(NC):
            r.prefix[h * NC + c] = acc.astype(BF16)
            rows = slice(c * C, (c + 1) * C)
            acc = acc + dot_tn(r.k[rows, head_lanes(h)], r.v[rows, head_lanes(h)])
        r.h_own[h] = acc
    r.h_y[y] = r.h_own[y]

    pl.semaphore_wait(barrier, NY + NZ + NH - 3)

    for o in range(NY):
        send(y != o, r.h_own.at[o], r.h_y.at[y], r.s_hy.at[o], r.r_hy.at[y], at_y(o))

    causal = lambda: lax.broadcasted_iota(jnp.int32, (C, C), 0) >= lax.broadcasted_iota(
        jnp.int32, (C, C), 1
    )
    anti = lambda: lax.broadcasted_iota(jnp.int32, (C, C), 0) <= lax.broadcasted_iota(
        jnp.int32, (C, C), 1
    )

    def local_step(c, carry):
        rows = chunk_rows(c)
        for h in range(HL):
            lanes = head_lanes(h)
            qc = r.q[rows, lanes]
            kept = jnp.where(causal(), dot_nt(qc, r.k[rows, lanes]), 0.0).astype(BF16)
            r.local[rows, lanes] = dot_nn(kept, r.v[rows, lanes]) + dot_nn(
                qc, r.prefix[h * NC + c]
            )
        return carry

    ins[2].wait()
    lax.fori_loop(0, 2, local_step, 0)

    for o in range(NY):
        receive(y != o, r.h_y.at[o], r.s_hy.at[o], r.r_hy.at[o], at_y(o))
    low = r.h_y[0] + r.h_y[1]
    r.a_own[...] = low
    r.t_own[...] = low + (r.h_y[2] + r.h_y[3])
    r.t_z[z] = r.t_own[sub_rows(z), :]
    for o in range(NZ):
        send(
            z != o,
            r.t_own.at[pl.ds(o * SUB, SUB), :],
            r.t_z.at[z],
            r.s_tz.at[o],
            r.r_tz.at[z],
            at_z(o),
        )
    for o in (1, 3):
        send(y != o, r.h_y.at[o - 1], r.b_all.at[0, y], r.s_by.at[0, o], r.r_by.at[0, y], at_y(o))
    for o in (2, 3):
        send(y != o, r.a_own, r.b_all.at[1, y], r.s_by.at[1, o], r.r_by.at[1, y], at_y(o))

    @pl.when(y_odd)
    def _():
        r.b_all[0, y] = r.h_y[y - 1]

    @pl.when(y_high)
    def _():
        r.b_all[1, y] = r.a_own[...]

    lax.fori_loop(2, NC, local_step, 0)

    for o in range(NZ):
        receive(z != o, r.t_z.at[o], r.s_tz.at[o], r.r_tz.at[o], at_z(o))
    low = r.t_z[0] + r.t_z[1]
    r.pair_z[0] = low
    r.pair_z[1] = r.t_z[4] + r.t_z[5]
    r.quad_z[...] = low + (r.t_z[2] + r.t_z[3])
    level_src = lambda b, o: [r.t_z.at[o - 1], r.pair_z.at[o // 4], r.quad_z][b]
    for b in (2, 1, 0):
        for o in range(NZ):
            if o >> b & 1:
                send(
                    z != o,
                    level_src(b, o),
                    r.b_own.at[b, sub_rows(z), :],
                    r.s_bz.at[b, o],
                    r.r_bz.at[b, z],
                    at_z(o),
                )

    @pl.when(zbit[0])
    def _():
        r.b_own[0, sub_rows(z), :] = r.t_z[z - 1]

    @pl.when(zbit[1])
    def _():
        r.b_own[1, sub_rows(z), :] = r.pair_z[z // 4]

    @pl.when(zbit[2])
    def _():
        r.b_own[2, sub_rows(z), :] = r.quad_z[...]

    ins[3].wait()
    for level in range(6):
        r.lam_rows[level * HL : (level + 1) * HL, :] = r.lam[level]
    r.lam_rows[6 * HL :, :] = jnp.zeros((D - 6 * HL, T), F32)
    for c in range(T // D):
        r.lam_cols[c * D : (c + 1) * D, :] = r.lam_rows[:, c * D : (c + 1) * D].T

    def spread_step(c, carry):
        rows = chunk_rows(c, D)
        cols = r.lam_cols[rows, :]
        for level in range(6):
            for h in range(HL):
                at = level * HL + h
                r.lam_wide[level, rows, head_lanes(h)] = jnp.broadcast_to(
                    cols[:, at : at + 1], (D, D)
                )
        return carry

    lax.fori_loop(0, T // D, spread_step, 0)

    for b in (2, 1, 0):
        for o in range(NZ):
            receive(
                zbit[b] & (z != o),
                r.b_own.at[b, pl.ds(o * SUB, SUB), :],
                r.s_bz.at[b, o],
                r.r_bz.at[b, o],
                at_z(o),
            )
        for o in range(NY):
            send(
                zbit[b] & (y != o),
                r.b_own.at[b],
                r.b_all.at[b + 2, y],
                r.s_ba.at[b, o],
                r.r_ba.at[b, y],
                at_y(o),
            )

    for b, there, sources in ((0, y_odd, None), (1, y_high, None)):
        for o in range(NY):
            receive(
                there & (y != o),
                r.b_all.at[b, o],
                r.s_by.at[b, o],
                r.r_by.at[b, o],
                at_y(o),
            )

    def take_bucket(b, there):
        @pl.when(there)
        def _():
            for h in range(HL):
                r.bcat[h, :, b * D : (b + 1) * D] = r.b_all[b, h].astype(BF16)

        @pl.when(jnp.logical_not(there))
        def _():
            for h in range(HL):
                r.bcat[h, :, b * D : (b + 1) * D] = jnp.zeros((D, D), BF16)

    take_bucket(0, y_odd)
    take_bucket(1, y_high)

    def first_step(c, carry):
        rows = chunk_rows(c)
        for h in range(HL):
            lanes = head_lanes(h)
            qc = r.q[rows, lanes]
            r.kept_t[h * NC + c] = jnp.where(anti(), dot_nt(r.k[rows, lanes], qc), 0.0).astype(
                BF16
            )
            two = dot_nn(qc, r.bcat[h, :, : 2 * D])
            r.reads[h, rows, : 2 * D] = two
            r.out[rows, lanes] = (
                r.lam_wide[0, rows, lanes] * r.local[rows, lanes]
                + r.lam_wide[1, rows, lanes] * two[:, :D]
                + r.lam_wide[2, rows, lanes] * two[:, D:]
            )
        return carry

    lax.fori_loop(0, NC, first_step, 0)

    for h in range(HL):
        for c in range(NC):
            r.q_t[h, :, c * C : (c + 1) * C] = r.q[c * C : (c + 1) * C, head_lanes(h)].T

    for b in (2, 1, 0):
        for o in range(NY):
            receive(
                zbit[b] & (y != o),
                r.b_all.at[b + 2, o],
                r.s_ba.at[b, o],
                r.r_ba.at[b, o],
                at_y(o),
            )

        @pl.when(zbit[b])
        def _(b=b):
            r.b_all[b + 2, y] = r.b_own[b]

        take_bucket(b + 2, zbit[b])

    ins[4].wait()
    ins[5].wait()

    def out_step(c, carry):
        rows = chunk_rows(c)
        squares = []
        inners = []
        for h in range(HL):
            lanes = head_lanes(h)
            three = dot_nn(r.q[rows, lanes], r.bcat[h, :, 2 * D :])
            r.reads[h, rows, 2 * D :] = three
            total = r.out[rows, lanes]
            for b in range(3):
                total = (
                    total + r.lam_wide[b + 3, rows, lanes] * three[:, b * D : (b + 1) * D]
                )
            r.out[rows, lanes] = total
            weighted = r.cot[rows, lanes].astype(F32) * r.gain[:, lanes]
            squares.append((total * total).astype(BF16))
            inners.append((total * weighted).astype(BF16))
        ones = jnp.ones((8, HL * D), BF16)
        r.stat_own[0:1, rows] = dot_nt(ones, jnp.concatenate(squares, axis=1))[0:1]
        r.stat_own[1:2, rows] = dot_nt(ones, jnp.concatenate(inners, axis=1))[0:1]
        return carry

    lax.fori_loop(0, NC, out_step, 0)

    for o in range(NH):
        send(
            head != o,
            r.stat_own.at[pl.ds(0, 2), :],
            r.stat_all.at[head, pl.ds(0, 2), :],
            r.s_st.at[o],
            r.r_st.at[head],
            at_head(o),
        )
    r.stat_all[head, 0:2, :] = r.stat_own[0:2, :]
    for o in range(NH):
        receive(
            head != o,
            r.stat_all.at[o, pl.ds(0, 2), :],
            r.s_st.at[o],
            r.r_st.at[o],
            at_head(o),
        )
    stats = r.stat_all[0, 0:2, :]
    for o in range(1, NH):
        stats = stats + r.stat_all[o, 0:2, :]
    count = HL * D * NH
    scale = lax.rsqrt(stats[0:1] * (1.0 / count) + EPS)
    pull = stats[1:2] * scale * scale * (1.0 / count)
    r.lam_rows[2:3, :] = scale
    r.lam_rows[3:4, :] = pull
    for c in range(T // D):
        r.stat_cols[c * D : (c + 1) * D, :] = r.lam_rows[:, c * D : (c + 1) * D].T

    r.gg_own[...] = jnp.zeros((8, HL * D), F32)

    def grad_step(c, carry):
        rows = chunk_rows(c, D)
        cols = r.stat_cols[rows, :]
        scale = jnp.broadcast_to(cols[:, 2:3], (D, D))
        pull = jnp.broadcast_to(cols[:, 3:4], (D, D))
        for h in range(HL):
            lanes = head_lanes(h)
            total = r.out[rows, lanes]
            normed = total * scale
            gain = r.gain[:, lanes]
            cot = r.cot[rows, lanes].astype(F32)
            r.mixed[rows, lanes] = (normed * gain).astype(BF16)
            r.gg_own[:, lanes] += jnp.sum((cot * normed).reshape(D // 8, 8, D), axis=0)
            grad = ((cot * gain - total * pull) * scale).astype(BF16)
            r.do[rows, lanes] = grad
            grad = grad.astype(F32)
            r.e[rows, lanes] = (r.lam_wide[0, rows, lanes] * grad).astype(BF16)
            for b in range(5):
                r.fcat[h, rows, b * D : (b + 1) * D] = (
                    r.lam_wide[b + 1, rows, lanes] * grad
                ).astype(BF16)
        return carry

    lax.fori_loop(0, T // D, grad_step, 0)

    mixed_copy = pltpu.make_async_copy(r.mixed, mixed_h, r.sem_out.at[0])
    mixed_copy.start()

    for h in range(HL):
        res = dot_nn(r.q_t[h], r.fcat[h])
        for b in range(5):
            r.db[b, h] = res[:, b * D : (b + 1) * D]
    for b in (2, 1, 0):
        for o in range(NY):
            send(
                zbit[b] & (y != o),
                r.db.at[b + 2, o],
                r.db_y.at[b + 2, y],
                r.s_db.at[b + 2, o],
                r.r_db.at[b + 2, y],
                at_y(o),
            )
    for b, there in ((0, y_odd), (1, y_high)):
        for o in range(NY):
            send(
                there & (y != o),
                r.db.at[b, o],
                r.db_y.at[b, y],
                r.s_db.at[b, o],
                r.r_db.at[b, y],
                at_y(o),
            )
    for b in range(5):
        r.db_y[b, y] = r.db[b, y]
    r.gg_own[0:1, :] = jnp.sum(r.gg_own[...], axis=0, keepdims=True)
    for o in range(NY):
        send(
            y != o,
            r.gg_own.at[pl.ds(0, 1), :],
            r.gg_y.at[y, pl.ds(0, 1), :],
            r.s_ggy.at[o],
            r.r_ggy.at[y],
            at_y(o),
        )
    r.gg_y[y, 0:1, :] = r.gg_own[0:1, :]

    def level_step(c, carry):
        rows = chunk_rows(c)
        pick = (
            lax.broadcasted_iota(jnp.int32, (8, HL * D), 1) // D
            == lax.broadcasted_iota(jnp.int32, (8, HL * D), 0)
        ).astype(BF16)
        grad = [r.do[rows, head_lanes(h)].astype(F32) for h in range(HL)]
        for level in range(6):
            parts = []
            for h in range(HL):
                if level == 0:
                    read = r.local[rows, head_lanes(h)]
                else:
                    read = r.reads[h, rows, (level - 1) * D : level * D]
                parts.append((grad[h] * read).astype(BF16))
            r.gl[level, :, rows] = dot_nt(pick, jnp.concatenate(parts, axis=1))[0:HL]
        return carry

    def query_step(c, carry):
        rows = chunk_rows(c)
        for h in range(HL):
            lanes = head_lanes(h)
            ec = r.e[rows, lanes]
            pair = jnp.where(causal(), dot_nt(ec, r.v[rows, lanes]), 0.0).astype(BF16)
            r.gq[rows, lanes] = (
                dot_nn(pair, r.k[rows, lanes])
                + dot_nt(ec, r.prefix[h * NC + c])
                + dot_nt(r.fcat[h, rows, :], r.bcat[h])
            ).astype(BF16)
        return carry

    lax.fori_loop(0, NC, query_step, 0)
    gq_copy = pltpu.make_async_copy(r.gq, gq_h, r.sem_out.at[1])
    gq_copy.start()

    for b in (2, 1, 0):
        for o in range(NY):
            receive(
                zbit[b] & (y != o),
                r.db_y.at[b + 2, o],
                r.s_db.at[b + 2, o],
                r.r_db.at[b + 2, o],
                at_y(o),
            )

        @pl.when(zbit[b])
        def _(b=b):
            total = r.db_y[b + 2, 0] + r.db_y[b + 2, 1] + (r.db_y[b + 2, 2] + r.db_y[b + 2, 3])
            r.u_own[b] = total
            r.u_z[b, z] = r.u_own[b, sub_rows(z), :]

        for o in range(NZ):
            send(
                zbit[b] & (z != o),
                r.u_own.at[b, pl.ds(o * SUB, SUB), :],
                r.u_z.at[b, z],
                r.s_uz.at[b, o],
                r.r_uz.at[b, z],
                at_z(o),
            )
    for o in range(NY):
        receive(
            y != o, r.gg_y.at[o, pl.ds(0, 1), :], r.s_ggy.at[o], r.r_ggy.at[o], at_y(o)
        )
    r.gg_mid[0:1, :] = (r.gg_y[0, 0:1, :] + r.gg_y[1, 0:1, :]) + (
        r.gg_y[2, 0:1, :] + r.gg_y[3, 0:1, :]
    )
    for o in range(NZ):
        send(
            z != o,
            r.gg_mid.at[pl.ds(0, 1), :],
            r.gg_z.at[z, pl.ds(0, 1), :],
            r.s_ggz.at[o],
            r.r_ggz.at[z],
            at_z(o),
        )
    r.gg_z[z, 0:1, :] = r.gg_mid[0:1, :]

    lax.fori_loop(0, NC, level_step, 0)
    gl_copy = pltpu.make_async_copy(r.gl, gl_h, r.sem_out.at[2])
    gl_copy.start()

    for b in (2, 1, 0):
        for o in range(NZ):
            if o >> b & 1:
                receive(z != o, r.u_z.at[b, o], r.s_uz.at[b, o], r.r_uz.at[b, o], at_z(o))
    quad = (r.u_z[2, 4] + r.u_z[2, 5]) + (r.u_z[2, 6] + r.u_z[2, 7])
    pair_low = r.u_z[1, 2] + r.u_z[1, 3]
    pair_high = r.u_z[1, 6] + r.u_z[1, 7]
    low = pair_low + quad
    r.g_z[0] = low + r.u_z[0, 1]
    r.g_z[1] = low
    r.g_z[2] = quad + r.u_z[0, 3]
    r.g_z[3] = quad
    r.g_z[4] = pair_high + r.u_z[0, 5]
    r.g_z[5] = pair_high
    r.g_z[6] = r.u_z[0, 7]
    r.g_z[7] = jnp.zeros((SUB, D), F32)
    for o in range(NZ):
        send(
            z != o, r.g_z.at[o], r.g_own.at[sub_rows(z), :], r.s_gz.at[o], r.r_gz.at[z], at_z(o)
        )
    r.g_own[sub_rows(z), :] = r.g_z[z]

    def key_step(c, carry):
        rows = chunk_rows(c)
        for h in range(HL):
            lanes = head_lanes(h)
            ec = r.e[rows, lanes]
            pair = jnp.where(anti(), dot_nt(r.v[rows, lanes], ec), 0.0).astype(BF16)
            r.local[rows, lanes] = dot_nn(pair, r.q[rows, lanes])
            r.out[rows, lanes] = dot_nn(r.kept_t[h * NC + c], ec)
            r.ds[h * NC + c] = dot_nn(r.q_t[h, :, rows], ec)
        return carry

    lax.fori_loop(0, 2, key_step, 0)

    for b, sources in ((0, (1, 3)), (1, (2, 3))):
        for o in sources:
            receive(y != o, r.db_y.at[b, o], r.s_db.at[b, o], r.r_db.at[b, o], at_y(o))
    for o in range(NZ):
        receive(
            z != o,
            r.g_own.at[pl.ds(o * SUB, SUB), :],
            r.s_gz.at[o],
            r.r_gz.at[o],
            at_z(o),
        )
    shared = r.g_own[...]
    upper = shared + (r.db_y[1, 2] + r.db_y[1, 3])
    r.dh_own[0] = upper + r.db_y[0, 1]
    r.dh_own[1] = upper
    r.dh_own[2] = shared + r.db_y[0, 3]
    r.dh_own[3] = shared
    for o in range(NY):
        send(y != o, r.dh_own.at[o], r.dh.at[y], r.s_dh.at[o], r.r_dh.at[y], at_y(o))
    r.dh[y] = r.dh_own[y]

    lax.fori_loop(2, NC, key_step, 0)

    for o in range(NZ):
        receive(
            z != o, r.gg_z.at[o, pl.ds(0, 1), :], r.s_ggz.at[o], r.r_ggz.at[o], at_z(o)
        )
    total = r.gg_z[0, 0:1, :]
    for o in range(1, NZ):
        total = total + r.gg_z[o, 0:1, :]
    r.gg[...] = total
    gg_copy = pltpu.make_async_copy(r.gg, gg_h, r.sem_out.at[3])
    gg_copy.start()

    for o in range(NY):
        receive(y != o, r.dh.at[o], r.s_dh.at[o], r.r_dh.at[o], at_y(o))

    for h in range(HL):
        lanes = head_lanes(h)
        acc = r.dh[h]
        for c in reversed(range(NC)):
            rows = slice(c * C, (c + 1) * C)
            half = acc.astype(BF16)
            r.gk[rows, lanes] = (r.local[rows, lanes] + dot_nt(r.v[rows, lanes], half)).astype(
                BF16
            )
            r.gv[rows, lanes] = (r.out[rows, lanes] + dot_nn(r.k[rows, lanes], half)).astype(
                BF16
            )
            acc = acc + r.ds[h * NC + c]
    gk_copy = pltpu.make_async_copy(r.gk, gk_h, r.sem_out.at[4])
    gv_copy = pltpu.make_async_copy(r.gv, gv_h, r.sem_out.at[5])
    gk_copy.start()
    gv_copy.start()

    for cond, make in sent:
        when(cond, lambda make=make: make().wait_send())
    for copy in (mixed_copy, gq_copy, gl_copy, gg_copy, gk_copy, gv_copy):
        copy.wait()


def body(query, key, value, level_coef, gain, cotangent):
    anywhere = pl.BlockSpec(memory_space=pl.ANY)
    wide = jax.ShapeDtypeStruct((T, HL * D), BF16)
    mixed, gq, gk, gv, gl, gg = pl.pallas_call(
        kernel,
        out_shape=(
            wide,
            wide,
            wide,
            wide,
            jax.ShapeDtypeStruct((6, HL, T), F32),
            jax.ShapeDtypeStruct((1, HL * D), F32),
        ),
        in_specs=[anywhere] * 6,
        out_specs=(anywhere,) * 6,
        scratch_shapes=list(SCRATCH.values()),
        compiler_params=pltpu.CompilerParams(
            collective_id=0, has_side_effects=True, vmem_limit_bytes=60 * 2**20
        ),
    )(query, key, value, level_coef, gain.reshape(1, -1), cotangent)
    return mixed, gq, gk, gv, gl, gg.reshape(-1)


def solution(mesh):
    placed = (
        P("seq", "head"),
        P("seq", "head"),
        P("seq", "head"),
        P(None, "head", "seq"),
        P("head"),
        P("seq", "head"),
    )
    return jax.shard_map(
        body,
        mesh=mesh,
        in_specs=placed,
        out_specs=(
            P("seq", "head"),
            P("seq", "head"),
            P("seq", "head"),
            P("seq", "head"),
            P(None, "head", "seq"),
            P("head"),
        ),
        check_vma=False,
    )
```

time: 240 us -> 81.4 us (0.34)
  waiting for transfers between devices: 102 us -> 0 us
  Pallas kernels: 0 us -> 71.5 us
  matrix products: 50 us -> 0 us
  starting transfers between devices: 38.9 us -> 0 us
  other arithmetic: 24.7 us -> 0 us
  local copies, waits for them, and re-layouts: 20.3 us -> 7.78 us
    ppermute x10 -> x0, waiting for transfers between devices: 96.4 us -> none  [from_partner(): return lax.ppermute(block, axis, route)]
    pallas_call x0 -> x1, Pallas kernels: none -> 71.5 us  [body(): pl.pallas_call(kernel, out_shape=(wide, wide, wide, wide, jax.ShapeDtypeS...]
    dot_general x12 -> x0, matrix products: 50 us -> none  [the longest x1 7.59 us: body(): jnp.einsum('the,lhef->lthf', q_three, bucket_half, preferred_element_type...]
    ppermute x10 -> x0, starting transfers between devices: 22.9 us -> none  [from_partner(): return lax.ppermute(block, axis, route)]
    all_to_all x3 -> x0, starting transfers between devices: 16 us -> none  [sent_to_all(): return lax.all_to_all(copies, axis, split_axis=0, concat_axis=0, tiled=True)]
    reduce_sum x6 -> x0, other arithmetic: 13.5 us -> none  [the longest x1 6.75 us: body(): grad_rest = jnp.sum(grad_float[None] * reads, axis=-1)]
    add x8 -> x0, other arithmetic: 8.09 us -> none  [the longest x4 7.02 us: body(): pending = pending[1:] + other[1:]]
    all_to_all x3 -> x0, waiting for transfers between devices: 5.16 us -> none  [sent_to_all(): return lax.all_to_all(copies, axis, split_axis=0, concat_axis=0, tiled=True)]
  transfers between devices with their start and end apart: 13 -> 0, of which waited for: 11 -> 0; matrix products, arithmetic and copies ran while one was open for 23% -> 0% of each run, Pallas kernels for 0% -> 0%
where the time goes in v1:
time: 81.4 us; the launch traced here: 80 us
  Pallas kernels  71.5 us (88%)
  local copies, waits for them, and re-layouts  7.78 us (10%)
    pallas_call x1, Pallas kernels, body(): pl.pallas_call(kernel, out_shape=(wide, wide, wide, wide, jax.ShapeDtypeS...  71.5 us
    unnamed x16, local copies, waits for them, and re-layouts  7.78 us

profile of v1, /device:TPU:6, one launch (start us, length us, event | category | flops | bytes accessed | tf_op | source)
XLA Modules:
  0.0 80.0 jit_solution(11860156967124624569)
XLA Ops:
  0.6 71.5 %shard_map.109 = (bf16[1024,512]{1,0:T(8,128)(2,1)}, bf16[1024,512]{1,0:T(8,128)(2,1)}, bf16[1024,512]{1,0:T(8,128)(2,1)}, bf16[1024,512]{1,0:T(8,128)(2,1)}, f32[6,4,1024]{2,1,0:T(4,128)}, /*index=5*/f32[1,512]{1,0:T(1,128)}) custom-call(bf16[1024,512]{1,0:T(8,128)(2,1)} %q_h.1, bf16[1024,512]{1,0:T(8,128)(2,1)} %k_h.1, bf16[1024,512]{1,0:T(8,128)(2,1)} %v_h.1, ...), custom_call_target="tpu_custom_call" | custom-call | tf_op jit(solution)/shard_map/pallas_call | solution.py:713
  72.2 0.0 copy-start.2
  72.2 2.4 %copy.18 = bf16[1024,512]{1,0:T(8,128)(2,1)} copy(bf16[1024,512]{1,0:T(8,128)(2,1)} %get-tuple-element.24) | data formatting | bytes 2097152
  74.5 0.0 copy-done.2
  74.5 0.0 copy-start.1
  74.6 1.0 %copy.19 = bf16[1024,512]{1,0:T(8,128)(2,1)} copy(bf16[1024,512]{1,0:T(8,128)(2,1)S(1)} %copy-done.2) | data formatting | bytes 2097152
  75.5 0.6 copy-done.1
  76.2 0.0 copy-start
  76.2 1.0 %copy.20 = bf16[1024,512]{1,0:T(8,128)(2,1)} copy(bf16[1024,512]{1,0:T(8,128)(2,1)S(1)} %copy-done.1) | data formatting | bytes 2097152
  77.1 0.6 copy-done
  77.8 0.0 copy-start.3
  77.8 1.0 %copy.21 = bf16[1024,512]{1,0:T(8,128)(2,1)} copy(bf16[1024,512]{1,0:T(8,128)(2,1)S(1)} %copy-done) | data formatting | bytes 2097152
  78.7 0.0 copy-done.3
  78.7 0.0 copy-start.4
  78.7 0.6 copy.22
  79.4 0.0 copy-done.4
  79.4 0.6 copy.23
Async XLA Ops:
  72.2 2.4 %copy-start.2 = (bf16[1024,512]{1,0:T(8,128)(2,1)S(1)}, bf16[1024,512]{1,0:T(8,128)(2,1)}, u32[]{:S(2)}) copy-start(bf16[1024,512]{1,0:T(8,128)(2,1)} %get-tuple-element.25) | copy-start | bytes 3145732
  74.5 1.6 %copy-start.1 = (bf16[1024,512]{1,0:T(8,128)(2,1)S(1)}, bf16[1024,512]{1,0:T(8,128)(2,1)}, u32[]{:S(2)}) copy-start(bf16[1024,512]{1,0:T(8,128)(2,1)} %get-tuple-element.26) | copy-start | bytes 3145732
  76.2 1.6 %copy-start = (bf16[1024,512]{1,0:T(8,128)(2,1)S(1)}, bf16[1024,512]{1,0:T(8,128)(2,1)}, u32[]{:S(2)}) copy-start(bf16[1024,512]{1,0:T(8,128)(2,1)} %get-tuple-element.27) | copy-start | bytes 3145732
  77.8 1.0 %copy-start.3 = (f32[6,4,1024]{2,1,0:T(4,128)S(1)}, f32[6,4,1024]{2,1,0:T(4,128)}, u32[]{:S(2)}) copy-start(f32[6,4,1024]{2,1,0:T(4,128)} %get-tuple-element.28) | copy-start | bytes 294916
  78.7 0.7 copy-start.4

commit v2 on v1

v2 whole, which is shorter than its diff:
```python
import jax
import jax.numpy as jnp
from jax import lax
from jax.experimental import pallas as pl
from jax.experimental.pallas import tpu as pltpu
from jax.sharding import PartitionSpec as P

EPS = 1e-06
F32 = jnp.float32
BF16 = jnp.bfloat16
MESH = pl.DeviceIdType.MESH

NY = 4
NZ = 8
NH = 8
HL = 4
D = 128
T = 1024
C = 256
NC = T // C
SUB = D // NZ


def dot_nn(a, b):
    return lax.dot_general(a, b, (((1,), (0,)), ((), ())), preferred_element_type=F32)


def dot_nt(a, b):
    return lax.dot_general(a, b, (((1,), (1,)), ((), ())), preferred_element_type=F32)


def dot_tn(a, b):
    return lax.dot_general(a, b, (((0,), (0,)), ((), ())), preferred_element_type=F32)


def head_lanes(h):
    if isinstance(h, int):
        return slice(h * D, (h + 1) * D)
    return pl.ds(pl.multiple_of(h * D, D), D)


def chunk_rows(c, size=C):
    return pl.ds(pl.multiple_of(c * size, size), size)


def when(cond, fn):
    if cond is True:
        fn()
    elif cond is not False:
        pl.when(cond)(fn)


SCRATCH = dict(
    q=pltpu.VMEM((T, HL * D), BF16),
    k=pltpu.VMEM((T, HL * D), BF16),
    v=pltpu.VMEM((T, HL * D), BF16),
    cot=pltpu.VMEM((T, HL * D), BF16),
    lam=pltpu.VMEM((6, HL, T), F32),
    gain=pltpu.VMEM((1, HL * D), F32),
    lam_rows=pltpu.VMEM((D, T), F32),
    lam_cols=pltpu.VMEM((T, D), F32),
    lam_wide=pltpu.VMEM((6, T, HL * D), F32),
    prefix=pltpu.VMEM((HL * NC, D, D), BF16),
    local=pltpu.VMEM((T, HL * D), F32),
    key_part=pltpu.VMEM((T, HL * D), F32),
    reads=pltpu.VMEM((HL, T, 5 * D), F32),
    out=pltpu.VMEM((T, HL * D), F32),
    kept_t=pltpu.VMEM((HL * NC, C, C), BF16),
    q_t=pltpu.VMEM((HL, D, T), BF16),
    bcat=pltpu.VMEM((HL, D, 5 * D), BF16),
    fcat=pltpu.VMEM((HL, T, 5 * D), BF16),
    e=pltpu.VMEM((T, HL * D), BF16),
    do=pltpu.VMEM((T, HL * D), BF16),
    ds=pltpu.VMEM((HL * NC, D, D), F32),
    stat_cols=pltpu.VMEM((T, D), F32),
    h_own=pltpu.VMEM((HL, D, D), F32),
    h_y=pltpu.VMEM((NY, D, D), F32),
    t_own=pltpu.VMEM((D, D), F32),
    a_own=pltpu.VMEM((D, D), F32),
    t_z=pltpu.VMEM((NZ, SUB, D), F32),
    pair_z=pltpu.VMEM((2, SUB, D), F32),
    quad_z=pltpu.VMEM((SUB, D), F32),
    b_own=pltpu.VMEM((3, D, D), F32),
    b_all=pltpu.VMEM((5, HL, D, D), F32),
    stat_own=pltpu.VMEM((8, T), F32),
    stat_all=pltpu.VMEM((NH, 8, T), F32),
    db=pltpu.VMEM((5, HL, D, D), F32),
    db_y=pltpu.VMEM((5, NY, D, D), F32),
    u_own=pltpu.VMEM((3, D, D), F32),
    u_z=pltpu.VMEM((3, NZ, SUB, D), F32),
    g_z=pltpu.VMEM((NZ, SUB, D), F32),
    g_own=pltpu.VMEM((D, D), F32),
    dh_own=pltpu.VMEM((NY, D, D), F32),
    dh=pltpu.VMEM((HL, D, D), F32),
    gg_own=pltpu.VMEM((8, HL * D), F32),
    gg_y=pltpu.VMEM((NY, 8, HL * D), F32),
    gg_mid=pltpu.VMEM((8, HL * D), F32),
    gg_z=pltpu.VMEM((NZ, 8, HL * D), F32),
    sem_in=pltpu.SemaphoreType.DMA((6,)),
    s_hy=pltpu.SemaphoreType.DMA((NY,)),
    r_hy=pltpu.SemaphoreType.DMA((NY,)),
    s_by=pltpu.SemaphoreType.DMA((2, NY)),
    r_by=pltpu.SemaphoreType.DMA((2, NY)),
    s_tz=pltpu.SemaphoreType.DMA((NZ,)),
    r_tz=pltpu.SemaphoreType.DMA((NZ,)),
    s_bz=pltpu.SemaphoreType.DMA((3, NZ)),
    r_bz=pltpu.SemaphoreType.DMA((3, NZ)),
    s_ba=pltpu.SemaphoreType.DMA((3, NY)),
    r_ba=pltpu.SemaphoreType.DMA((3, NY)),
    s_st=pltpu.SemaphoreType.DMA((NH,)),
    r_st=pltpu.SemaphoreType.DMA((NH,)),
    s_db=pltpu.SemaphoreType.DMA((5, NY)),
    r_db=pltpu.SemaphoreType.DMA((5, NY)),
    s_uz=pltpu.SemaphoreType.DMA((3, NZ)),
    r_uz=pltpu.SemaphoreType.DMA((3, NZ)),
    s_gz=pltpu.SemaphoreType.DMA((NZ,)),
    r_gz=pltpu.SemaphoreType.DMA((NZ,)),
    s_dh=pltpu.SemaphoreType.DMA((NY,)),
    r_dh=pltpu.SemaphoreType.DMA((NY,)),
    s_ggy=pltpu.SemaphoreType.DMA((NY,)),
    r_ggy=pltpu.SemaphoreType.DMA((NY,)),
    s_ggz=pltpu.SemaphoreType.DMA((NZ,)),
    r_ggz=pltpu.SemaphoreType.DMA((NZ,)),
)


class Refs:
    def __init__(self, refs):
        for name, ref in zip(SCRATCH, refs, strict=True):
            setattr(self, name, ref)


def sub_rows(z):
    return pl.ds(pl.multiple_of(z * SUB, SUB), SUB)


Y_TURNS = (1, 3, 2)
Z_TURNS = (4, 3, 5, 2, 6, 1, 7)
HEAD_TURNS = (4, 3, 5, 2, 6, 1, 7)


def kernel(q_h, k_h, v_h, lam_h, gain_h, cot_h, mixed_o, gq_o, gk_o, gv_o, gl_o, gg_o, *refs):
    r = Refs(refs)
    seq = lax.axis_index("seq")
    head = lax.axis_index("head")
    y = lax.rem(seq, NY)
    z = seq // NY
    bit = lambda x, b: lax.rem(x // 2**b, 2) == 1
    zbit = [bit(z, b) for b in range(3)]
    y_odd = bit(y, 0)
    y_high = y >= 2

    at_y = lambda other: (z * NY + other, head)
    at_z = lambda other: (other * NY + y, head)
    at_head = lambda other: (seq, other)
    ahead = lambda me, turn, count: lax.rem(me + turn, count)
    behind = lambda me, turn, count: lax.rem(me + count - turn, count)

    sent = []

    def send(cond, src, dst, s_sem, r_sem, device):
        def make():
            return pltpu.make_async_remote_copy(
                src_ref=src,
                dst_ref=dst,
                send_sem=s_sem,
                recv_sem=r_sem,
                device_id=device,
                device_id_type=MESH,
            )

        when(cond, lambda: make().start())
        sent.append((cond, make))

    def receive(cond, dst, s_sem, r_sem, device):
        def wait():
            pltpu.make_async_remote_copy(
                src_ref=dst,
                dst_ref=dst,
                send_sem=s_sem,
                recv_sem=r_sem,
                device_id=device,
                device_id_type=MESH,
            ).wait_recv()

        when(cond, wait)

    barrier = pltpu.get_barrier_semaphore()

    def greet(device):
        pl.semaphore_signal(barrier, inc=1, device_id=device, device_id_type=MESH)

    for d in Z_TURNS:
        greet(at_z(ahead(z, d, NZ)))
    for d in HEAD_TURNS:
        greet(at_head(ahead(head, d, NH)))
    for d in Y_TURNS:
        greet(at_y(ahead(y, d, NY)))

    ins = [
        pltpu.make_async_copy(src, dst, r.sem_in.at[i])
        for i, (src, dst) in enumerate(
            [(k_h, r.k), (v_h, r.v), (q_h, r.q), (lam_h, r.lam), (cot_h, r.cot), (gain_h, r.gain)]
        )
    ]
    for copy in ins:
        copy.start()

    ins[0].wait()
    ins[1].wait()
    for i, d in enumerate(Y_TURNS + (0,)):
        h = ahead(y, d, NY)
        lanes = head_lanes(h)
        acc = jnp.zeros((D, D), F32)
        for c in range(NC):
            r.prefix[h * NC + c] = acc.astype(BF16)
            rows = slice(c * C, (c + 1) * C)
            acc = acc + dot_tn(r.k[rows, lanes], r.v[rows, lanes])
        if d == 0:
            r.h_y[y] = acc
        else:
            r.h_own[h] = acc
            if i == 0:
                pl.semaphore_wait(barrier, NY + NZ + NH - 3)
            send(True, r.h_own.at[h], r.h_y.at[y], r.s_hy.at[d], r.r_hy.at[d], at_y(h))

    causal = lambda: lax.broadcasted_iota(jnp.int32, (C, C), 0) >= lax.broadcasted_iota(
        jnp.int32, (C, C), 1
    )
    anti = lambda: lax.broadcasted_iota(jnp.int32, (C, C), 0) <= lax.broadcasted_iota(
        jnp.int32, (C, C), 1
    )

    def local_step(c, carry):
        rows = chunk_rows(c)
        for h in range(HL):
            lanes = head_lanes(h)
            qc = r.q[rows, lanes]
            kept = jnp.where(causal(), dot_nt(qc, r.k[rows, lanes]), 0.0).astype(BF16)
            r.local[rows, lanes] = dot_nn(kept, r.v[rows, lanes]) + dot_nn(
                qc, r.prefix[h * NC + c]
            )
        return carry

    def spread_step(c, carry):
        rows = chunk_rows(c, D)
        cols = r.lam_cols[rows, :]
        for level in range(6):
            for h in range(HL):
                at = level * HL + h
                r.lam_wide[level, rows, head_lanes(h)] = jnp.broadcast_to(
                    cols[:, at : at + 1], (D, D)
                )
        return carry

    ins[2].wait()
    lax.fori_loop(0, NC, local_step, 0)
    ins[3].wait()
    for level in range(6):
        r.lam_rows[level * HL : (level + 1) * HL, :] = r.lam[level]
    r.lam_rows[6 * HL :, :] = jnp.zeros((D - 6 * HL, T), F32)
    for c in range(T // D):
        r.lam_cols[c * D : (c + 1) * D, :] = r.lam_rows[:, c * D : (c + 1) * D].T
    lax.fori_loop(0, 2, spread_step, 0)

    for d in Y_TURNS:
        o = behind(y, d, NY)
        receive(True, r.h_y.at[o], r.s_hy.at[d], r.r_hy.at[d], at_y(o))
    low = r.h_y[0] + r.h_y[1]
    r.a_own[...] = low
    r.t_own[...] = low + (r.h_y[2] + r.h_y[3])
    for d in Z_TURNS:
        o = ahead(z, d, NZ)
        send(
            True,
            r.t_own.at[sub_rows(o), :],
            r.t_z.at[z],
            r.s_tz.at[d],
            r.r_tz.at[d],
            at_z(o),
        )
    r.t_z[z] = r.t_own[sub_rows(z), :]
    for o in (1, 3):
        send(y != o, r.h_y.at[o - 1], r.b_all.at[0, y], r.s_by.at[0, o], r.r_by.at[0, y], at_y(o))
    for o in (2, 3):
        send(y != o, r.a_own, r.b_all.at[1, y], r.s_by.at[1, o], r.r_by.at[1, y], at_y(o))

    @pl.when(y_odd)
    def _():
        r.b_all[0, y] = r.h_y[y - 1]

    @pl.when(y_high)
    def _():
        r.b_all[1, y] = r.a_own[...]

    lax.fori_loop(2, T // D, spread_step, 0)

    for d in Z_TURNS:
        o = behind(z, d, NZ)
        receive(True, r.t_z.at[o], r.s_tz.at[d], r.r_tz.at[d], at_z(o))
    low = r.t_z[0] + r.t_z[1]
    r.pair_z[0] = low
    r.pair_z[1] = r.t_z[4] + r.t_z[5]
    r.quad_z[...] = low + (r.t_z[2] + r.t_z[3])
    for b in (2, 1, 0):
        for d in Z_TURNS:
            o = ahead(z, d, NZ)
            src = (r.t_z.at[lax.rem(o + NZ - 1, NZ)], r.pair_z.at[o // 4], r.quad_z)[b]
            send(
                bit(o, b),
                src,
                r.b_own.at[b, sub_rows(z), :],
                r.s_bz.at[b, d],
                r.r_bz.at[b, d],
                at_z(o),
            )

    @pl.when(zbit[0])
    def _():
        r.b_own[0, sub_rows(z), :] = r.t_z[z - 1]

    @pl.when(zbit[1])
    def _():
        r.b_own[1, sub_rows(z), :] = r.pair_z[z // 4]

    @pl.when(zbit[2])
    def _():
        r.b_own[2, sub_rows(z), :] = r.quad_z[...]

    def take_bucket(b, there):
        @pl.when(there)
        def _():
            for h in range(HL):
                r.bcat[h, :, b * D : (b + 1) * D] = r.b_all[b, h].astype(BF16)

        @pl.when(jnp.logical_not(there))
        def _():
            for h in range(HL):
                r.bcat[h, :, b * D : (b + 1) * D] = jnp.zeros((D, D), BF16)

    for b, there in ((0, y_odd), (1, y_high)):
        for o in range(NY):
            receive(
                there & (y != o),
                r.b_all.at[b, o],
                r.s_by.at[b, o],
                r.r_by.at[b, o],
                at_y(o),
            )
        take_bucket(b, there)

    def first_step(c, carry):
        rows = chunk_rows(c)
        for h in range(HL):
            lanes = head_lanes(h)
            two = dot_nn(r.q[rows, lanes], r.bcat[h, :, : 2 * D])
            r.reads[h, rows, : 2 * D] = two
            r.out[rows, lanes] = (
                r.lam_wide[0, rows, lanes] * r.local[rows, lanes]
                + r.lam_wide[1, rows, lanes] * two[:, :D]
                + r.lam_wide[2, rows, lanes] * two[:, D:]
            )
        return carry

    for b in (2, 1, 0):
        for d in Z_TURNS:
            o = behind(z, d, NZ)
            receive(
                zbit[b],
                r.b_own.at[b, sub_rows(o), :],
                r.s_bz.at[b, d],
                r.r_bz.at[b, d],
                at_z(o),
            )
        for d in Y_TURNS:
            o = ahead(y, d, NY)
            send(
                zbit[b],
                r.b_own.at[b],
                r.b_all.at[b + 2, y],
                r.s_ba.at[b, d],
                r.r_ba.at[b, d],
                at_y(o),
            )

        @pl.when(zbit[b])
        def _(b=b):
            r.b_all[b + 2, y] = r.b_own[b]

    lax.fori_loop(0, NC, first_step, 0)
    ins[4].wait()
    ins[5].wait()

    for b in (2, 1, 0):
        for d in Y_TURNS:
            o = behind(y, d, NY)
            receive(
                zbit[b],
                r.b_all.at[b + 2, o],
                r.s_ba.at[b, d],
                r.r_ba.at[b, d],
                at_y(o),
            )
        take_bucket(b + 2, zbit[b])

    def out_step(c, carry):
        rows = chunk_rows(c)
        squares = []
        inners = []
        for h in range(HL):
            lanes = head_lanes(h)
            three = dot_nn(r.q[rows, lanes], r.bcat[h, :, 2 * D :])
            r.reads[h, rows, 2 * D :] = three
            total = r.out[rows, lanes]
            for b in range(3):
                total = (
                    total + r.lam_wide[b + 3, rows, lanes] * three[:, b * D : (b + 1) * D]
                )
            r.out[rows, lanes] = total
            weighted = r.cot[rows, lanes].astype(F32) * r.gain[:, lanes]
            squares.append((total * total).astype(BF16))
            inners.append((total * weighted).astype(BF16))
        ones = jnp.ones((8, HL * D), BF16)
        r.stat_own[0:1, rows] = dot_nt(ones, jnp.concatenate(squares, axis=1))[0:1]
        r.stat_own[1:2, rows] = dot_nt(ones, jnp.concatenate(inners, axis=1))[0:1]
        return carry

    lax.fori_loop(0, NC, out_step, 0)

    for d in HEAD_TURNS:
        o = ahead(head, d, NH)
        send(
            True,
            r.stat_own.at[pl.ds(0, 2), :],
            r.stat_all.at[head, pl.ds(0, 2), :],
            r.s_st.at[d],
            r.r_st.at[d],
            at_head(o),
        )
    r.stat_all[head, 0:2, :] = r.stat_own[0:2, :]

    for h in range(HL):
        for c in range(NC):
            r.q_t[h, :, c * C : (c + 1) * C] = r.q[c * C : (c + 1) * C, head_lanes(h)].T

    def kept_step(c, carry):
        rows = chunk_rows(c)
        for h in range(HL):
            lanes = head_lanes(h)
            r.kept_t[h * NC + c] = jnp.where(
                anti(), dot_nt(r.k[rows, lanes], r.q[rows, lanes]), 0.0
            ).astype(BF16)
        return carry

    lax.fori_loop(0, NC, kept_step, 0)

    for d in HEAD_TURNS:
        o = behind(head, d, NH)
        receive(
            True,
            r.stat_all.at[o, pl.ds(0, 2), :],
            r.s_st.at[d],
            r.r_st.at[d],
            at_head(o),
        )
    stats = r.stat_all[0, 0:2, :]
    for o in range(1, NH):
        stats = stats + r.stat_all[o, 0:2, :]
    count = HL * D * NH
    scale = lax.rsqrt(stats[0:1] * (1.0 / count) + EPS)
    pull = stats[1:2] * scale * scale * (1.0 / count)
    r.lam_rows[2:3, :] = scale
    r.lam_rows[3:4, :] = pull
    for c in range(T // D):
        r.stat_cols[c * D : (c + 1) * D, :] = r.lam_rows[:, c * D : (c + 1) * D].T

    r.gg_own[...] = jnp.zeros((8, HL * D), F32)

    def grad_step(h):
        lanes = head_lanes(h)

        def step(c, carry):
            rows = chunk_rows(c, D)
            cols = r.stat_cols[rows, :]
            scale = jnp.broadcast_to(cols[:, 2:3], (D, D))
            pull = jnp.broadcast_to(cols[:, 3:4], (D, D))
            total = r.out[rows, lanes]
            normed = total * scale
            gain = r.gain[:, lanes]
            cot = r.cot[rows, lanes].astype(F32)
            mixed_o[rows, lanes] = (normed * gain).astype(BF16)
            r.gg_own[:, lanes] += jnp.sum((cot * normed).reshape(D // 8, 8, D), axis=0)
            grad = ((cot * gain - total * pull) * scale).astype(BF16)
            r.do[rows, lanes] = grad
            grad = grad.astype(F32)
            r.e[rows, lanes] = (r.lam_wide[0, rows, lanes] * grad).astype(BF16)
            for b in range(5):
                r.fcat[h, rows, b * D : (b + 1) * D] = (
                    r.lam_wide[b + 1, rows, lanes] * grad
                ).astype(BF16)
            return carry

        lax.fori_loop(0, T // D, step, 0)

    for d in Y_TURNS + (0,):
        h = ahead(y, d, NY)
        grad_step(h)
        res = dot_nn(r.q_t[h], r.fcat[h, :, 2 * D :])
        for b in range(3):
            piece = res[:, b * D : (b + 1) * D]
            if d == 0:
                r.db_y[b + 2, y] = piece
            else:
                r.db[b + 2, h] = piece
        if d:
            for b in (2, 1, 0):
                send(
                    zbit[b],
                    r.db.at[b + 2, h],
                    r.db_y.at[b + 2, y],
                    r.s_db.at[b + 2, d],
                    r.r_db.at[b + 2, d],
                    at_y(h),
                )
    for h in range(HL):
        res = dot_nn(r.q_t[h], r.fcat[h, :, : 2 * D])
        for b in range(2):
            r.db[b, h] = res[:, b * D : (b + 1) * D]
    r.gg_own[0:1, :] = jnp.sum(r.gg_own[...], axis=0, keepdims=True)

    def level_step(c, carry):
        rows = chunk_rows(c)
        pick = (
            lax.broadcasted_iota(jnp.int32, (8, HL * D), 1) // D
            == lax.broadcasted_iota(jnp.int32, (8, HL * D), 0)
        ).astype(BF16)
        grad = [r.do[rows, head_lanes(h)].astype(F32) for h in range(HL)]
        for level in range(6):
            parts = []
            for h in range(HL):
                if level == 0:
                    read = r.local[rows, head_lanes(h)]
                else:
                    read = r.reads[h, rows, (level - 1) * D : level * D]
                parts.append((grad[h] * read).astype(BF16))
            gl_o[level, :, rows] = dot_nt(pick, jnp.concatenate(parts, axis=1))[0:HL]
        return carry

    def query_step(c, carry):
        rows = chunk_rows(c)
        for h in range(HL):
            lanes = head_lanes(h)
            ec = r.e[rows, lanes]
            pair = jnp.where(causal(), dot_nt(ec, r.v[rows, lanes]), 0.0).astype(BF16)
            gq_o[rows, lanes] = (
                dot_nn(pair, r.k[rows, lanes])
                + dot_nt(ec, r.prefix[h * NC + c])
                + dot_nt(r.fcat[h, rows, :], r.bcat[h])
            ).astype(BF16)
        return carry

    def key_step(c, carry):
        rows = chunk_rows(c)
        for h in range(HL):
            lanes = head_lanes(h)
            ec = r.e[rows, lanes]
            pair = jnp.where(anti(), dot_nt(r.v[rows, lanes], ec), 0.0).astype(BF16)
            r.key_part[rows, lanes] = dot_nn(pair, r.q[rows, lanes])
            r.out[rows, lanes] = dot_nn(r.kept_t[h * NC + c], ec)
            r.ds[h * NC + c] = dot_nn(r.q_t[h, :, rows], ec)
        return carry

    lax.fori_loop(0, NC, query_step, 0)
    lax.fori_loop(0, 3, key_step, 0)

    for b in (2, 1, 0):
        for d in Y_TURNS:
            o = behind(y, d, NY)
            receive(
                zbit[b],
                r.db_y.at[b + 2, o],
                r.s_db.at[b + 2, d],
                r.r_db.at[b + 2, d],
                at_y(o),
            )

        @pl.when(zbit[b])
        def _(b=b):
            total = r.db_y[b + 2, 0] + r.db_y[b + 2, 1] + (r.db_y[b + 2, 2] + r.db_y[b + 2, 3])
            r.u_own[b] = total
            r.u_z[b, z] = r.u_own[b, sub_rows(z), :]

        for d in Z_TURNS:
            o = ahead(z, d, NZ)
            send(
                zbit[b],
                r.u_own.at[b, sub_rows(o), :],
                r.u_z.at[b, z],
                r.s_uz.at[b, d],
                r.r_uz.at[b, d],
                at_z(o),
            )
    for b, there in ((0, y_odd), (1, y_high)):
        for d in Y_TURNS:
            o = ahead(y, d, NY)
            send(
                there,
                r.db.at[b, o],
                r.db_y.at[b, y],
                r.s_db.at[b, d],
                r.r_db.at[b, d],
                at_y(o),
            )
        r.db_y[b, y] = r.db[b, y]
    for d in Y_TURNS:
        o = ahead(y, d, NY)
        send(
            True,
            r.gg_own.at[pl.ds(0, 1), :],
            r.gg_y.at[y, pl.ds(0, 1), :],
            r.s_ggy.at[d],
            r.r_ggy.at[d],
            at_y(o),
        )
    r.gg_y[y, 0:1, :] = r.gg_own[0:1, :]

    lax.fori_loop(3, NC, key_step, 0)
    lax.fori_loop(0, 2, level_step, 0)

    for b in (2, 1, 0):
        for d in Z_TURNS:
            o = behind(z, d, NZ)
            receive(bit(o, b), r.u_z.at[b, o], r.s_uz.at[b, d], r.r_uz.at[b, d], at_z(o))
    quad = (r.u_z[2, 4] + r.u_z[2, 5]) + (r.u_z[2, 6] + r.u_z[2, 7])
    pair_low = r.u_z[1, 2] + r.u_z[1, 3]
    pair_high = r.u_z[1, 6] + r.u_z[1, 7]
    low = pair_low + quad
    r.g_z[0] = low + r.u_z[0, 1]
    r.g_z[1] = low
    r.g_z[2] = quad + r.u_z[0, 3]
    r.g_z[3] = quad
    r.g_z[4] = pair_high + r.u_z[0, 5]
    r.g_z[5] = pair_high
    r.g_z[6] = r.u_z[0, 7]
    r.g_z[7] = jnp.zeros((SUB, D), F32)
    for d in Z_TURNS:
        o = ahead(z, d, NZ)
        send(
            True,
            r.g_z.at[o],
            r.g_own.at[sub_rows(z), :],
            r.s_gz.at[d],
            r.r_gz.at[d],
            at_z(o),
        )
    r.g_own[sub_rows(z), :] = r.g_z[z]

    for d in Y_TURNS:
        o = behind(y, d, NY)
        receive(True, r.gg_y.at[o, pl.ds(0, 1), :], r.s_ggy.at[d], r.r_ggy.at[d], at_y(o))
    r.gg_mid[0:1, :] = (r.gg_y[0, 0:1, :] + r.gg_y[1, 0:1, :]) + (
        r.gg_y[2, 0:1, :] + r.gg_y[3, 0:1, :]
    )
    for d in Z_TURNS:
        o = ahead(z, d, NZ)
        send(
            True,
            r.gg_mid.at[pl.ds(0, 1), :],
            r.gg_z.at[z, pl.ds(0, 1), :],
            r.s_ggz.at[d],
            r.r_ggz.at[d],
            at_z(o),
        )
    r.gg_z[z, 0:1, :] = r.gg_mid[0:1, :]

    lax.fori_loop(2, NC, level_step, 0)

    for b, sources in ((0, (1, 3)), (1, (2, 3))):
        for d in Y_TURNS:
            o = behind(y, d, NY)
            there = bit(o, b)
            receive(there, r.db_y.at[b, o], r.s_db.at[b, d], r.r_db.at[b, d], at_y(o))
    for d in Z_TURNS:
        o = behind(z, d, NZ)
        receive(True, r.g_own.at[sub_rows(o), :], r.s_gz.at[d], r.r_gz.at[d], at_z(o))
    shared = r.g_own[...]
    upper = shared + (r.db_y[1, 2] + r.db_y[1, 3])
    r.dh_own[0] = upper + r.db_y[0, 1]
    r.dh_own[1] = upper
    r.dh_own[2] = shared + r.db_y[0, 3]
    r.dh_own[3] = shared
    for d in Y_TURNS:
        o = ahead(y, d, NY)
        send(True, r.dh_own.at[o], r.dh.at[y], r.s_dh.at[d], r.r_dh.at[d], at_y(o))
    r.dh[y] = r.dh_own[y]

    for d in (0,) + Y_TURNS:
        h = behind(y, d, NY)
        lanes = head_lanes(h)
        if d:
            receive(True, r.dh.at[h], r.s_dh.at[d], r.r_dh.at[d], at_y(h))
        acc = r.dh[h]
        for c in reversed(range(NC)):
            rows = slice(c * C, (c + 1) * C)
            half = acc.astype(BF16)
            gk_o[rows, lanes] = (
                r.key_part[rows, lanes] + dot_nt(r.v[rows, lanes], half)
            ).astype(BF16)
            gv_o[rows, lanes] = (r.out[rows, lanes] + dot_nn(r.k[rows, lanes], half)).astype(
                BF16
            )
            acc = acc + r.ds[h * NC + c]

    for d in Z_TURNS:
        o = behind(z, d, NZ)
        receive(True, r.gg_z.at[o, pl.ds(0, 1), :], r.s_ggz.at[d], r.r_ggz.at[d], at_z(o))
    total = r.gg_z[0, 0:1, :]
    for o in range(1, NZ):
        total = total + r.gg_z[o, 0:1, :]
    gg_o[...] = total

    for cond, make in sent:
        when(cond, lambda make=make: make().wait_send())


def store_kernel(*refs):
    ins, outs, sem = refs[:6], refs[6:12], refs[12]
    copies = [pltpu.make_async_copy(a, b, sem.at[i]) for i, (a, b) in enumerate(zip(ins, outs))]
    for copy in copies:
        copy.start()
    for copy in copies:
        copy.wait()


def body(query, key, value, level_coef, gain, cotangent):
    anywhere = pl.BlockSpec(memory_space=pl.ANY)
    inside = pl.BlockSpec(memory_space=pltpu.VMEM)
    shapes = [((T, HL * D), BF16)] * 4 + [((6, HL, T), F32), ((1, HL * D), F32)]
    results = pl.pallas_call(
        kernel,
        out_shape=tuple(pltpu.VMEM(*shape) for shape in shapes),
        in_specs=[anywhere] * 6,
        out_specs=(inside,) * 6,
        scratch_shapes=list(SCRATCH.values()),
        compiler_params=pltpu.CompilerParams(
            collective_id=0, has_side_effects=True, vmem_limit_bytes=54 * 2**20
        ),
    )(query, key, value, level_coef, gain.reshape(1, -1), cotangent)
    mixed, gq, gk, gv, gl, gg = pl.pallas_call(
        store_kernel,
        out_shape=tuple(jax.ShapeDtypeStruct(*shape) for shape in shapes),
        in_specs=[inside] * 6,
        out_specs=(anywhere,) * 6,
        scratch_shapes=[pltpu.SemaphoreType.DMA((6,))],
        compiler_params=pltpu.CompilerParams(vmem_limit_bytes=2**20),
    )(*results)
    return mixed, gq, gk, gv, gl, gg.reshape(-1)


def solution(mesh):
    placed = (
        P("seq", "head"),
        P("seq", "head"),
        P("seq", "head"),
        P(None, "head", "seq"),
        P("head"),
        P("seq", "head"),
    )
    return jax.shard_map(
        body,
        mesh=mesh,
        in_specs=placed,
        out_specs=(
            P("seq", "head"),
            P("seq", "head"),
            P("seq", "head"),
            P("seq", "head"),
            P(None, "head", "seq"),
            P("head"),
        ),
        check_vma=False,
    )
```

time: 81.4 us -> 70.8 us (0.87); the launches traced: 80 us -> 70.7 us
  local copies, waits for them, and re-layouts: 7.78 us -> 0 us
  Pallas kernels: 71.5 us -> 70.1 us
    unnamed x16 -> x0, local copies, waits for them, and re-layouts: 7.78 us -> none
    pallas_call x1 -> x2, Pallas kernels: 71.5 us -> 70.1 us  [the longest x1 68 us: body(): pl.pallas_call(kernel, out_shape=tuple((pltpu.VMEM(*shape) for shape in s...]
where the time goes in v2:
time: 70.8 us; the launch traced here: 70.7 us
  Pallas kernels  70.1 us (99%)
    pallas_call x1, Pallas kernels, body(): pl.pallas_call(kernel, out_shape=tuple((pltpu.VMEM(*shape) for shape in s...  68 us
    pallas_call x1, Pallas kernels, body(): pl.pallas_call(store_kernel, out_shape=tuple((jax.ShapeDtypeStruct(*shape...  2.08 us

profile of v2, /device:TPU:6, one launch (start us, length us, event | category | flops | bytes accessed | tf_op | source)
XLA Modules:
  0.0 70.7 jit_solution(968383164303932164)
XLA Ops:
  0.6 68.0 %shard_map.109 = (bf16[1024,512]{1,0:T(8,128)(2,1)S(1)}, bf16[1024,512]{1,0:T(8,128)(2,1)S(1)}, bf16[1024,512]{1,0:T(8,128)(2,1)S(1)}, bf16[1024,512]{1,0:T(8,12...) custom-call(bf16[1024,512]{1,0:T(8,128)(2,1)} %q_h.1, bf16[1024,512]{1,0:T(8,128)(2,1)} %k_h.1, ...), custom_call_target="tpu_custom_call" | custom-call | tf_op jit(solution)/shard_map/pallas_call | solution.py:739
  68.6 2.1 %shard_map.110 = (bf16[1024,512]{1,0:T(8,128)(2,1)}, bf16[1024,512]{1,0:T(8,128)(2,1)}, bf16[1024,512]{1,0:T(8,128)(2,1)}, bf16[1024,512]{1,0:T(8,128)(2,1)}, f32[6,4,1024]{2,1,0:T(4,128)}, /*index=5*/f32[1,512]{1,0:T(1,128)}) custom-call(bf16[1024,512]{1,0:T(8,128)(2,1)S(1)} %get-tuple-element.18.refs_0_, bf16[1024,512]{1,0:T(8,128)(2,1)S(1)} %get-tuple-element.19.refs_1_, ...), custom_call_target="tpu_custom_call" | custom-call | tf_op jit(solution)/shard_map/pallas_call | solution.py:749

commit v3 on v2

--- a/solution.py
+++ b/solution.py
@@ -68,6 +68,7 @@
     kept_t=pltpu.VMEM((HL * NC, C, C), BF16),
     q_t=pltpu.VMEM((HL, D, T), BF16),
     bcat=pltpu.VMEM((HL, D, 5 * D), BF16),
+    bhigh=pltpu.VMEM((HL, 2 * D, D), BF16),
     fcat=pltpu.VMEM((HL, T, 5 * D), BF16),
     e=pltpu.VMEM((T, HL * D), BF16),
     do=pltpu.VMEM((T, HL * D), BF16),
@@ -90,6 +91,7 @@
     u_z=pltpu.VMEM((3, NZ, SUB, D), F32),
     g_z=pltpu.VMEM((NZ, SUB, D), F32),
     g_own=pltpu.VMEM((D, D), F32),
+    u0_in=pltpu.VMEM((D, D), F32),
     dh_own=pltpu.VMEM((NY, D, D), F32),
     dh=pltpu.VMEM((HL, D, D), F32),
     gg_own=pltpu.VMEM((8, HL * D), F32),
@@ -97,6 +99,11 @@
     gg_mid=pltpu.VMEM((8, HL * D), F32),
     gg_z=pltpu.VMEM((NZ, 8, HL * D), F32),
     sem_in=pltpu.SemaphoreType.DMA((6,)),
+    ring=pltpu.SemaphoreType.REGULAR((2,)),
+    s_t0=pltpu.SemaphoreType.DMA((1,)),
+    r_t0=pltpu.SemaphoreType.DMA((1,)),
+    s_u0=pltpu.SemaphoreType.DMA((1,)),
+    r_u0=pltpu.SemaphoreType.DMA((1,)),
     s_hy=pltpu.SemaphoreType.DMA((NY,)),
     r_hy=pltpu.SemaphoreType.DMA((NY,)),
     s_by=pltpu.SemaphoreType.DMA((2, NY)),
@@ -147,6 +154,7 @@
     z = seq // NY
     bit = lambda x, b: lax.rem(x // 2**b, 2) == 1
     zbit = [bit(z, b) for b in range(3)]
+    z_even = lax.rem(z, 2) == 0
     y_odd = bit(y, 0)
     y_high = y >= 2
 
@@ -185,29 +193,40 @@
 
         when(cond, wait)
 
-    barrier = pltpu.get_barrier_semaphore()
-
-    def greet(device):
-        pl.semaphore_signal(barrier, inc=1, device_id=device, device_id_type=MESH)
-
-    for d in Z_TURNS:
-        greet(at_z(ahead(z, d, NZ)))
-    for d in HEAD_TURNS:
-        greet(at_head(ahead(head, d, NH)))
-    for d in Y_TURNS:
-        greet(at_y(ahead(y, d, NY)))
-
     ins = [
         pltpu.make_async_copy(src, dst, r.sem_in.at[i])
         for i, (src, dst) in enumerate(
             [(k_h, r.k), (v_h, r.v), (q_h, r.q), (lam_h, r.lam), (cot_h, r.cot), (gain_h, r.gain)]
         )
     ]
-    for copy in ins:
+    for copy in ins[:2]:
         copy.start()
+
+    barrier = pltpu.get_barrier_semaphore()
+
+    def greet(device):
+        pl.semaphore_signal(barrier, inc=1, device_id=device, device_id_type=MESH)
+
+    for d in (1, NZ - 1):
+        greet(at_z(ahead(z, d, NZ)))
+    for d in Y_TURNS:
+        greet(at_y(ahead(y, d, NY)))
+    for d in HEAD_TURNS:
+        greet(at_head(ahead(head, d, NH)))
+
+    def pass_on(step, apart):
+        for d in (apart, NZ - apart):
+            pl.semaphore_signal(
+                r.ring.at[step],
+                inc=1,
+                device_id=at_z(ahead(z, d, NZ)),
+                device_id_type=MESH,
+            )
 
     ins[0].wait()
     ins[1].wait()
+    for copy in ins[2:]:
+        copy.start()
     for i, d in enumerate(Y_TURNS + (0,)):
         h = ahead(y, d, NY)
         lanes = head_lanes(h)
@@ -221,7 +240,7 @@
         else:
             r.h_own[h] = acc
             if i == 0:
-                pl.semaphore_wait(barrier, NY + NZ + NH - 3)
+                pl.semaphore_wait(barrier, NY + NH)
             send(True, r.h_own.at[h], r.h_y.at[y], r.s_hy.at[d], r.r_hy.at[d], at_y(h))
 
     causal = lambda: lax.broadcasted_iota(jnp.int32, (C, C), 0) >= lax.broadcasted_iota(
@@ -254,7 +273,11 @@
         return carry
 
     ins[2].wait()
-    lax.fori_loop(0, NC, local_step, 0)
+    pass_on(0, 1)
+    lax.fori_loop(0, 2, local_step, 0)
+    pl.semaphore_wait(r.ring.at[0], 2)
+    pass_on(1, 2)
+    lax.fori_loop(2, NC, local_step, 0)
     ins[3].wait()
     for level in range(6):
         r.lam_rows[level * HL : (level + 1) * HL, :] = r.lam[level]
@@ -269,6 +292,7 @@
     low = r.h_y[0] + r.h_y[1]
     r.a_own[...] = low
     r.t_own[...] = low + (r.h_y[2] + r.h_y[3])
+    pl.semaphore_wait(r.ring.at[1], 2)
     for d in Z_TURNS:
         o = ahead(z, d, NZ)
         send(
@@ -280,6 +304,8 @@
             at_z(o),
         )
     r.t_z[z] = r.t_own[sub_rows(z), :]
+    up, down = ahead(z, 1, NZ), behind(z, 1, NZ)
+    send(z_even, r.t_own, r.b_own.at[0], r.s_t0.at[0], r.r_t0.at[0], at_z(up))
     for o in (1, 3):
         send(y != o, r.h_y.at[o - 1], r.b_all.at[0, y], r.s_by.at[0, o], r.r_by.at[0, y], at_y(o))
     for o in (2, 3):
@@ -295,83 +321,7 @@
 
     lax.fori_loop(2, T // D, spread_step, 0)
 
-    for d in Z_TURNS:
-        o = behind(z, d, NZ)
-        receive(True, r.t_z.at[o], r.s_tz.at[d], r.r_tz.at[d], at_z(o))
-    low = r.t_z[0] + r.t_z[1]
-    r.pair_z[0] = low
-    r.pair_z[1] = r.t_z[4] + r.t_z[5]
-    r.quad_z[...] = low + (r.t_z[2] + r.t_z[3])
-    for b in (2, 1, 0):
-        for d in Z_TURNS:
-            o = ahead(z, d, NZ)
-            src = (r.t_z.at[lax.rem(o + NZ - 1, NZ)], r.pair_z.at[o // 4], r.quad_z)[b]
-            send(
-                bit(o, b),
-                src,
-                r.b_own.at[b, sub_rows(z), :],
-                r.s_bz.at[b, d],
-                r.r_bz.at[b, d],
-                at_z(o),
-            )
-
-    @pl.when(zbit[0])
-    def _():
-        r.b_own[0, sub_rows(z), :] = r.t_z[z - 1]
-
-    @pl.when(zbit[1])
-    def _():
-        r.b_own[1, sub_rows(z), :] = r.pair_z[z // 4]
-
-    @pl.when(zbit[2])
-    def _():
-        r.b_own[2, sub_rows(z), :] = r.quad_z[...]
-
-    def take_bucket(b, there):
-        @pl.when(there)
-        def _():
-            for h in range(HL):
-                r.bcat[h, :, b * D : (b + 1) * D] = r.b_all[b, h].astype(BF16)
-
-        @pl.when(jnp.logical_not(there))
-        def _():
-            for h in range(HL):
-                r.bcat[h, :, b * D : (b + 1) * D] = jnp.zeros((D, D), BF16)
-
-    for b, there in ((0, y_odd), (1, y_high)):
-        for o in range(NY):
-            receive(
-                there & (y != o),
-                r.b_all.at[b, o],
-                r.s_by.at[b, o],
-                r.r_by.at[b, o],
-                at_y(o),
-            )
-        take_bucket(b, there)
-
-    def first_step(c, carry):
-        rows = chunk_rows(c)
-        for h in range(HL):
-            lanes = head_lanes(h)
-            two = dot_nn(r.q[rows, lanes], r.bcat[h, :, : 2 * D])
-            r.reads[h, rows, : 2 * D] = two
-            r.out[rows, lanes] = (
-                r.lam_wide[0, rows, lanes] * r.local[rows, lanes]
-                + r.lam_wide[1, rows, lanes] * two[:, :D]
-                + r.lam_wide[2, rows, lanes] * two[:, D:]
-            )
-        return carry
-
-    for b in (2, 1, 0):
-        for d in Z_TURNS:
-            o = behind(z, d, NZ)
-            receive(
-                zbit[b],
-                r.b_own.at[b, sub_rows(o), :],
-                r.s_bz.at[b, d],
-                r.r_bz.at[b, d],
-                at_z(o),
-            )
+    def share_bucket(b):
         for d in Y_TURNS:
             o = ahead(y, d, NY)
             send(
@@ -384,14 +334,10 @@
             )
 
         @pl.when(zbit[b])
-        def _(b=b):
+        def _():
             r.b_all[b + 2, y] = r.b_own[b]
 
-    lax.fori_loop(0, NC, first_step, 0)
-    ins[4].wait()
-    ins[5].wait()
-
-    for b in (2, 1, 0):
+    def receive_bucket(b):
         for d in Y_TURNS:
             o = behind(y, d, NY)
             receive(
@@ -403,21 +349,122 @@
             )
         take_bucket(b + 2, zbit[b])
 
+    receive(zbit[0], r.b_own.at[0], r.s_t0.at[0], r.r_t0.at[0], at_z(down))
+    share_bucket(0)
+
+    for d in Z_TURNS:
+        o = behind(z, d, NZ)
+        receive(True, r.t_z.at[o], r.s_tz.at[d], r.r_tz.at[d], at_z(o))
+    low = r.t_z[0] + r.t_z[1]
+    r.pair_z[0] = low
+    r.pair_z[1] = r.t_z[4] + r.t_z[5]
+    r.quad_z[...] = low + (r.t_z[2] + r.t_z[3])
+    for b in (2, 1):
+        for d in Z_TURNS:
+            o = ahead(z, d, NZ)
+            src = (None, r.pair_z.at[o // 4], r.quad_z)[b]
+            send(
+                bit(o, b),
+                src,
+                r.b_own.at[b, sub_rows(z), :],
+                r.s_bz.at[b, d],
+                r.r_bz.at[b, d],
+                at_z(o),
+            )
+
+    @pl.when(zbit[1])
+    def _():
+        r.b_own[1, sub_rows(z), :] = r.pair_z[z // 4]
+
+    @pl.when(zbit[2])
+    def _():
+        r.b_own[2, sub_rows(z), :] = r.quad_z[...]
+
+    def take_bucket(b, there):
+        @pl.when(there)
+        def _():
+            for h in range(HL):
+                half = r.b_all[b, h].astype(BF16)
+                r.bcat[h, :, b * D : (b + 1) * D] = half
+                if b >= 3:
+                    r.bhigh[h, (b - 3) * D : (b - 2) * D, :] = half
+
+        @pl.when(jnp.logical_not(there))
+        def _():
+            for h in range(HL):
+                r.bcat[h, :, b * D : (b + 1) * D] = jnp.zeros((D, D), BF16)
+                if b >= 3:
+                    r.bhigh[h, (b - 3) * D : (b - 2) * D, :] = jnp.zeros((D, D), BF16)
+
+    def first_step(c, carry):
+        rows = chunk_rows(c)
+        for h in range(HL):
+            lanes = head_lanes(h)
+            three = dot_nn(r.q[rows, lanes], r.bcat[h, :, : 3 * D])
+            r.reads[h, rows, : 3 * D] = three
+            total = r.lam_wide[0, rows, lanes] * r.local[rows, lanes]
+            for b in range(3):
+                total = (
+                    total + r.lam_wide[b + 1, rows, lanes] * three[:, b * D : (b + 1) * D]
+                )
+            r.out[rows, lanes] = total
+            qf = r.q[rows, lanes].astype(F32)
+            for b in range(2):
+                r.fcat[h, rows, b * D : (b + 1) * D] = (
+                    r.lam_wide[b + 4, rows, lanes] * qf
+                ).astype(BF16)
+            r.key_part[rows, lanes] = r.cot[rows, lanes].astype(F32) * r.gain[:, lanes]
+        return carry
+
+    for b in (2, 1):
+        for d in Z_TURNS:
+            o = behind(z, d, NZ)
+            receive(
+                zbit[b],
+                r.b_own.at[b, sub_rows(o), :],
+                r.s_bz.at[b, d],
+                r.r_bz.at[b, d],
+                at_z(o),
+            )
+        share_bucket(b)
+
+    for b, there in ((0, y_odd), (1, y_high)):
+        for o in range(NY):
+            receive(
+                there & (y != o),
+                r.b_all.at[b, o],
+                r.s_by.at[b, o],
+                r.r_by.at[b, o],
+                at_y(o),
+            )
+        take_bucket(b, there)
+    receive_bucket(0)
+    ins[4].wait()
+    ins[5].wait()
+
+    lax.fori_loop(0, NC, first_step, 0)
+
+    def kept_step(c, carry):
+        rows = chunk_rows(c)
+        for h in range(HL):
+            lanes = head_lanes(h)
+            r.kept_t[h * NC + c] = jnp.where(
+                anti(), dot_nt(r.k[rows, lanes], r.q[rows, lanes]), 0.0
+            ).astype(BF16)
+        return carry
+
+    for b in (2, 1):
+        receive_bucket(b)
+
     def out_step(c, carry):
         rows = chunk_rows(c)
         squares = []
         inners = []
         for h in range(HL):
             lanes = head_lanes(h)
-            three = dot_nn(r.q[rows, lanes], r.bcat[h, :, 2 * D :])
-            r.reads[h, rows, 2 * D :] = three
-            total = r.out[rows, lanes]
-            for b in range(3):
-                total = (
-                    total + r.lam_wide[b + 3, rows, lanes] * three[:, b * D : (b + 1) * D]
-                )
+            total = r.out[rows, lanes] + dot_nn(r.fcat[h, rows, : 2 * D], r.bhigh[h])
             r.out[rows, lanes] = total
-            weighted = r.cot[rows, lanes].astype(F32) * r.gain[:, lanes]
+            weighted = r.key_part[rows, lanes]
             squares.append((total * total).astype(BF16))
             inners.append((total * weighted).astype(BF16))
         ones = jnp.ones((8, HL * D), BF16)
@@ -443,15 +490,13 @@
         for c in range(NC):
             r.q_t[h, :, c * C : (c + 1) * C] = r.q[c * C : (c + 1) * C, head_lanes(h)].T
 
-    def kept_step(c, carry):
+    def high_reads_step(c, carry):
         rows = chunk_rows(c)
         for h in range(HL):
-            lanes = head_lanes(h)
-            r.kept_t[h * NC + c] = jnp.where(
-                anti(), dot_nt(r.k[rows, lanes], r.q[rows, lanes]), 0.0
-            ).astype(BF16)
-        return carry
-
+            r.reads[h, rows, 3 * D :] = dot_nn(r.q[rows, head_lanes(h)], r.bcat[h, :, 3 * D :])
+        return carry
+
+    lax.fori_loop(0, NC, high_reads_step, 0)
     lax.fori_loop(0, NC, kept_step, 0)
 
     for d in HEAD_TURNS:
@@ -476,7 +521,7 @@
 
     r.gg_own[...] = jnp.zeros((8, HL * D), F32)
 
-    def grad_step(h):
+    def high_grad_step(h):
         lanes = head_lanes(h)
 
         def step(c, carry):
@@ -484,48 +529,81 @@
             cols = r.stat_cols[rows, :]
             scale = jnp.broadcast_to(cols[:, 2:3], (D, D))
             pull = jnp.broadcast_to(cols[:, 3:4], (D, D))
-            total = r.out[rows, lanes]
-            normed = total * scale
-            gain = r.gain[:, lanes]
-            cot = r.cot[rows, lanes].astype(F32)
-            mixed_o[rows, lanes] = (normed * gain).astype(BF16)
-            r.gg_own[:, lanes] += jnp.sum((cot * normed).reshape(D // 8, 8, D), axis=0)
-            grad = ((cot * gain - total * pull) * scale).astype(BF16)
+            grad = ((r.key_part[rows, lanes] - r.out[rows, lanes] * pull) * scale).astype(BF16)
             r.do[rows, lanes] = grad
             grad = grad.astype(F32)
-            r.e[rows, lanes] = (r.lam_wide[0, rows, lanes] * grad).astype(BF16)
-            for b in range(5):
+            for b in (3, 4):
                 r.fcat[h, rows, b * D : (b + 1) * D] = (
                     r.lam_wide[b + 1, rows, lanes] * grad
                 ).astype(BF16)
             return carry
 
-        lax.fori_loop(0, T // D, step, 0)
+        lax.fori_loop(0, T // D, step, 0, unroll=2)
+
+    def rest_step(c, carry):
+        rows = chunk_rows(c, D)
+        scale = jnp.broadcast_to(r.stat_cols[rows, 2:3], (D, D))
+        for h in range(HL):
+            lanes = head_lanes(h)
+            normed = r.out[rows, lanes] * scale
+            mixed_o[rows, lanes] = (normed * r.gain[:, lanes]).astype(BF16)
+            cot = r.cot[rows, lanes].astype(F32)
+            r.gg_own[:, lanes] += jnp.sum((cot * normed).reshape(D // 8, 8, D), axis=0)
+            grad = r.do[rows, lanes].astype(F32)
+            r.e[rows, lanes] = (r.lam_wide[0, rows, lanes] * grad).astype(BF16)
+            for b in range(3):
+                r.fcat[h, rows, b * D : (b + 1) * D] = (
+                    r.lam_wide[b + 1, rows, lanes] * grad
+                ).astype(BF16)
+        return carry
+
+    def send_grad(level, d, o, there):
+        send(
+            there,
+            r.db.at[level, o],
+            r.db_y.at[level, y],
+            r.s_db.at[level, d],
+            r.r_db.at[level, d],
+            at_y(o),
+        )
+
+    def receive_grad(level, there):
+        for d in Y_TURNS:
+            o = behind(y, d, NY)
+            receive(
+                there(o),
+                r.db_y.at[level, o],
+                r.s_db.at[level, d],
+                r.r_db.at[level, d],
+                at_y(o),
+            )
 
     for d in Y_TURNS + (0,):
         h = ahead(y, d, NY)
-        grad_step(h)
-        res = dot_nn(r.q_t[h], r.fcat[h, :, 2 * D :])
-        for b in range(3):
-            piece = res[:, b * D : (b + 1) * D]
+        high_grad_step(h)
+        res = dot_nn(r.q_t[h], r.fcat[h, :, 3 * D :])
+        for b in (1, 2):
+            piece = res[:, (b - 1) * D : b * D]
             if d == 0:
                 r.db_y[b + 2, y] = piece
             else:
                 r.db[b + 2, h] = piece
         if d:
-            for b in (2, 1, 0):
-                send(
-                    zbit[b],
-                    r.db.at[b + 2, h],
-                    r.db_y.at[b + 2, y],
-                    r.s_db.at[b + 2, d],
-                    r.r_db.at[b + 2, d],
-                    at_y(h),
-                )
-    for h in range(HL):
-        res = dot_nn(r.q_t[h], r.fcat[h, :, : 2 * D])
-        for b in range(2):
-            r.db[b, h] = res[:, b * D : (b + 1) * D]
+            for b in (2, 1):
+                send_grad(b + 2, d, h, zbit[b])
+    lax.fori_loop(0, T // D, rest_step, 0)
+    for d in Y_TURNS + (0,):
+        h = ahead(y, d, NY)
+        res = dot_nn(r.q_t[h], r.fcat[h, :, : 3 * D])
+        for b in range(3):
+            piece = res[:, b * D : (b + 1) * D]
+            if d == 0:
+                r.db_y[b, y] = piece
+            else:
+                r.db[b, h] = piece
+        if d:
+            for b, there in ((2, zbit[0]), (1, y_high), (0, y_odd)):
+                send_grad(b, d, h, there)
     r.gg_own[0:1, :] = jnp.sum(r.gg_own[...], axis=0, keepdims=True)
 
     def level_step(c, carry):
@@ -571,23 +649,17 @@
         return carry
 
     lax.fori_loop(0, NC, query_step, 0)
-    lax.fori_loop(0, 3, key_step, 0)
-
-    for b in (2, 1, 0):
-        for d in Y_TURNS:
-            o = behind(y, d, NY)
-            receive(
-                zbit[b],
-                r.db_y.at[b + 2, o],
-                r.s_db.at[b + 2, d],
-                r.r_db.at[b + 2, d],
-                at_y(o),
-            )
+    lax.fori_loop(0, 2, key_step, 0)
+
+    def sum_over_y(level):
+        return (r.db_y[level, 0] + r.db_y[level, 1]) + (r.db_y[level, 2] + r.db_y[level, 3])
+
+    for b in (2, 1):
+        receive_grad(b + 2, lambda o: zbit[b])
 
         @pl.when(zbit[b])
         def _(b=b):
-            total = r.db_y[b + 2, 0] + r.db_y[b + 2, 1] + (r.db_y[b + 2, 2] + r.db_y[b + 2, 3])
-            r.u_own[b] = total
+            r.u_own[b] = sum_over_y(b + 2)
             r.u_z[b, z] = r.u_own[b, sub_rows(z), :]
 
         for d in Z_TURNS:
@@ -600,18 +672,6 @@
                 r.r_uz.at[b, d],
                 at_z(o),
             )
-    for b, there in ((0, y_odd), (1, y_high)):
-        for d in Y_TURNS:
-            o = ahead(y, d, NY)
-            send(
-                there,
-                r.db.at[b, o],
-                r.db_y.at[b, y],
-                r.s_db.at[b, d],
-                r.r_db.at[b, d],
-                at_y(o),
-            )
-        r.db_y[b, y] = r.db[b, y]
     for d in Y_TURNS:
         o = ahead(y, d, NY)
         send(
@@ -624,10 +684,18 @@
         )
     r.gg_y[y, 0:1, :] = r.gg_own[0:1, :]
 
-    lax.fori_loop(3, NC, key_step, 0)
-    lax.fori_loop(0, 2, level_step, 0)
-
-    for b in (2, 1, 0):
+    lax.fori_loop(2, NC, key_step, 0)
+
+    receive_grad(2, lambda o: zbit[0])
+
+    @pl.when(zbit[0])
+    def _():
+        r.u_own[0] = sum_over_y(2)
+
+    send(zbit[0], r.u_own.at[0], r.u0_in, r.s_u0.at[0], r.r_u0.at[0], at_z(down))
+    lax.fori_loop(0, 1, level_step, 0)
+
+    for b in (2, 1):
         for d in Z_TURNS:
             o = behind(z, d, NZ)
             receive(bit(o, b), r.u_z.at[b, o], r.s_uz.at[b, d], r.r_uz.at[b, d], at_z(o))
@@ -635,25 +703,30 @@
     pair_low = r.u_z[1, 2] + r.u_z[1, 3]
     pair_high = r.u_z[1, 6] + r.u_z[1, 7]
     low = pair_low + quad
-    r.g_z[0] = low + r.u_z[0, 1]
+    r.g_z[0] = low
     r.g_z[1] = low
-    r.g_z[2] = quad + r.u_z[0, 3]
+    r.g_z[2] = quad
     r.g_z[3] = quad
-    r.g_z[4] = pair_high + r.u_z[0, 5]
+    r.g_z[4] = pair_high
     r.g_z[5] = pair_high
-    r.g_z[6] = r.u_z[0, 7]
-    r.g_z[7] = jnp.zeros((SUB, D), F32)
     for d in Z_TURNS:
         o = ahead(z, d, NZ)
         send(
-            True,
+            o < 6,
             r.g_z.at[o],
             r.g_own.at[sub_rows(z), :],
             r.s_gz.at[d],
             r.r_gz.at[d],
             at_z(o),
         )
-    r.g_own[sub_rows(z), :] = r.g_z[z]
+
+    @pl.when(z < 6)
+    def _():
+        r.g_own[sub_rows(z), :] = r.g_z[z]
+
+    @pl.when(z >= 6)
+    def _():
+        r.g_own[...] = jnp.zeros((D, D), F32)
 
     for d in Y_TURNS:
         o = behind(y, d, NY)
@@ -673,16 +746,19 @@
         )
     r.gg_z[z, 0:1, :] = r.gg_mid[0:1, :]
 
-    lax.fori_loop(2, NC, level_step, 0)
-
-    for b, sources in ((0, (1, 3)), (1, (2, 3))):
-        for d in Y_TURNS:
-            o = behind(y, d, NY)
-            there = bit(o, b)
-            receive(there, r.db_y.at[b, o], r.s_db.at[b, d], r.r_db.at[b, d], at_y(o))
+    lax.fori_loop(1, NC, level_step, 0)
+
+    for b in range(2):
+        receive_grad(b, lambda o: bit(o, b))
+    receive(z_even, r.u0_in, r.s_u0.at[0], r.r_u0.at[0], at_z(up))
     for d in Z_TURNS:
         o = behind(z, d, NZ)
-        receive(True, r.g_own.at[sub_rows(o), :], r.s_gz.at[d], r.r_gz.at[d], at_z(o))
+        receive(z < 6, r.g_own.at[sub_rows(o), :], r.s_gz.at[d], r.r_gz.at[d], at_z(o))
+
+    @pl.when(z_even)
+    def _():
+        r.g_own[...] += r.u0_in[...]
+
     shared = r.g_own[...]
     upper = shared + (r.db_y[1, 2] + r.db_y[1, 3])
     r.dh_own[0] = upper + r.db_y[0, 1]

time: 70.8 us -> 67.1 us (0.948)
  Pallas kernels: 70.1 us -> 66.2 us
    pallas_call x1, Pallas kernels: 68 us -> 64.1 us  [body(): pl.pallas_call(kernel, out_shape=tuple((pltpu.VMEM(*shape) for shape in s...]
where the time goes in v3:
time: 67.1 us; the launch traced here: 66.8 us
  Pallas kernels  66.2 us (99%)
    pallas_call x1, Pallas kernels, body(): pl.pallas_call(kernel, out_shape=tuple((pltpu.VMEM(*shape) for shape in s...  64.1 us
    pallas_call x1, Pallas kernels, body(): pl.pallas_call(store_kernel, out_shape=tuple((jax.ShapeDtypeStruct(*shape...  2.08 us

profile of v3, /device:TPU:6, one launch (start us, length us, event | category | flops | bytes accessed | tf_op | source)
XLA Modules:
  0.0 66.8 jit_solution(11004861129633174110)
XLA Ops:
  0.6 64.1 %shard_map.109 = (bf16[1024,512]{1,0:T(8,128)(2,1)S(1)}, bf16[1024,512]{1,0:T(8,128)(2,1)S(1)}, bf16[1024,512]{1,0:T(8,128)(2,1)S(1)}, bf16[1024,512]{1,0:T(8,12...) custom-call(bf16[1024,512]{1,0:T(8,128)(2,1)} %q_h.1, bf16[1024,512]{1,0:T(8,128)(2,1)} %k_h.1, ...), custom_call_target="tpu_custom_call" | custom-call | tf_op jit(solution)/shard_map/pallas_call | solution.py:815
  64.8 2.1 %shard_map.110 = (bf16[1024,512]{1,0:T(8,128)(2,1)}, bf16[1024,512]{1,0:T(8,128)(2,1)}, bf16[1024,512]{1,0:T(8,128)(2,1)}, bf16[1024,512]{1,0:T(8,128)(2,1)}, f32[6,4,1024]{2,1,0:T(4,128)}, /*index=5*/f32[1,512]{1,0:T(1,128)}) custom-call(bf16[1024,512]{1,0:T(8,128)(2,1)S(1)} %get-tuple-element.18.refs_0_, bf16[1024,512]{1,0:T(8,128)(2,1)S(1)} %get-tuple-element.19.refs_1_, ...), custom_call_target="tpu_custom_call" | custom-call | tf_op jit(solution)/shard_map/pallas_call | solution.py:825

commit v4 on v3

--- a/solution.py
+++ b/solution.py
@@ -18,7 +18,8 @@
 T = 1024
 C = 256
 NC = T // C
-SUB = D // NZ
+NQ = 4
+SUB = D // NQ
 
 
 def dot_nn(a, b):
@@ -78,8 +79,8 @@
     h_y=pltpu.VMEM((NY, D, D), F32),
     t_own=pltpu.VMEM((D, D), F32),
     a_own=pltpu.VMEM((D, D), F32),
-    t_z=pltpu.VMEM((NZ, SUB, D), F32),
-    pair_z=pltpu.VMEM((2, SUB, D), F32),
+    t_z=pltpu.VMEM((NQ, SUB, D), F32),
+    pair_z=pltpu.VMEM((SUB, D), F32),
     quad_z=pltpu.VMEM((SUB, D), F32),
     b_own=pltpu.VMEM((3, D, D), F32),
     b_all=pltpu.VMEM((5, HL, D, D), F32),
@@ -88,8 +89,9 @@
     db=pltpu.VMEM((5, HL, D, D), F32),
     db_y=pltpu.VMEM((5, NY, D, D), F32),
     u_own=pltpu.VMEM((3, D, D), F32),
-    u_z=pltpu.VMEM((3, NZ, SUB, D), F32),
-    g_z=pltpu.VMEM((NZ, SUB, D), F32),
+    u_z=pltpu.VMEM((3, NQ, SUB, D), F32),
+    g_z=pltpu.VMEM((2, SUB, D), F32),
+    g_in=pltpu.VMEM((2, D, D), F32),
     g_own=pltpu.VMEM((D, D), F32),
     u0_in=pltpu.VMEM((D, D), F32),
     dh_own=pltpu.VMEM((NY, D, D), F32),
@@ -98,7 +100,8 @@
     gg_y=pltpu.VMEM((NY, 8, HL * D), F32),
     gg_mid=pltpu.VMEM((8, HL * D), F32),
     gg_z=pltpu.VMEM((NZ, 8, HL * D), F32),
-    sem_in=pltpu.SemaphoreType.DMA((6,)),
+    sem_in=pltpu.SemaphoreType.DMA((4,)),
+    sem_kv=pltpu.SemaphoreType.DMA((2, HL)),
     ring=pltpu.SemaphoreType.REGULAR((2,)),
     s_t0=pltpu.SemaphoreType.DMA((1,)),
     r_t0=pltpu.SemaphoreType.DMA((1,)),
@@ -108,20 +111,20 @@
     r_hy=pltpu.SemaphoreType.DMA((NY,)),
     s_by=pltpu.SemaphoreType.DMA((2, NY)),
     r_by=pltpu.SemaphoreType.DMA((2, NY)),
-    s_tz=pltpu.SemaphoreType.DMA((NZ,)),
-    r_tz=pltpu.SemaphoreType.DMA((NZ,)),
-    s_bz=pltpu.SemaphoreType.DMA((3, NZ)),
-    r_bz=pltpu.SemaphoreType.DMA((3, NZ)),
+    s_tz=pltpu.SemaphoreType.DMA((NQ,)),
+    r_tz=pltpu.SemaphoreType.DMA((NQ,)),
+    s_bz=pltpu.SemaphoreType.DMA((3, NQ)),
+    r_bz=pltpu.SemaphoreType.DMA((3, NQ)),
     s_ba=pltpu.SemaphoreType.DMA((3, NY)),
     r_ba=pltpu.SemaphoreType.DMA((3, NY)),
     s_st=pltpu.SemaphoreType.DMA((NH,)),
     r_st=pltpu.SemaphoreType.DMA((NH,)),
     s_db=pltpu.SemaphoreType.DMA((5, NY)),
     r_db=pltpu.SemaphoreType.DMA((5, NY)),
-    s_uz=pltpu.SemaphoreType.DMA((3, NZ)),
-    r_uz=pltpu.SemaphoreType.DMA((3, NZ)),
-    s_gz=pltpu.SemaphoreType.DMA((NZ,)),
-    r_gz=pltpu.SemaphoreType.DMA((NZ,)),
+    s_uz=pltpu.SemaphoreType.DMA((3, NQ)),
+    r_uz=pltpu.SemaphoreType.DMA((3, NQ)),
+    s_gz=pltpu.SemaphoreType.DMA((2, NQ)),
+    r_gz=pltpu.SemaphoreType.DMA((2, NQ)),
     s_dh=pltpu.SemaphoreType.DMA((NY,)),
     r_dh=pltpu.SemaphoreType.DMA((NY,)),
     s_ggy=pltpu.SemaphoreType.DMA((NY,)),
@@ -141,8 +144,10 @@
     return pl.ds(pl.multiple_of(z * SUB, SUB), SUB)
 
 
-Y_TURNS = (1, 3, 2)
+Y_TURNS = (2, 1, 3)
+Y_ARRIVALS = (1, 3, 2)
 Z_TURNS = (4, 3, 5, 2, 6, 1, 7)
+Q_TURNS = (3, 2, 1)
 HEAD_TURNS = (4, 3, 5, 2, 6, 1, 7)
 
 
@@ -155,6 +160,9 @@
     bit = lambda x, b: lax.rem(x // 2**b, 2) == 1
     zbit = [bit(z, b) for b in range(3)]
     z_even = lax.rem(z, 2) == 0
+    zi = lax.rem(z, NQ)
+    quad = z // NQ
+    at_quad = lambda other: ((quad * NQ + other) * NY + y, head)
     y_odd = bit(y, 0)
     y_high = y >= 2
 
@@ -179,6 +187,11 @@
 
         when(cond, lambda: make().start())
         sent.append((cond, make))
+
+    def drain():
+        for cond, make in sent:
+            when(cond, lambda make=make: make().wait_send())
+        sent.clear()
 
     def receive(cond, dst, s_sem, r_sem, device):
         def wait():
@@ -193,14 +206,19 @@
 
         when(cond, wait)
 
+    kv = {}
+    for d in Y_TURNS + (0,):
+        lanes = head_lanes(ahead(y, d, NY))
+        kv[d] = [
+            pltpu.make_async_copy(src.at[:, lanes], dst.at[:, lanes], r.sem_kv.at[i, d])
+            for i, (src, dst) in enumerate([(k_h, r.k), (v_h, r.v)])
+        ]
+        for copy in kv[d]:
+            copy.start()
     ins = [
         pltpu.make_async_copy(src, dst, r.sem_in.at[i])
-        for i, (src, dst) in enumerate(
-            [(k_h, r.k), (v_h, r.v), (q_h, r.q), (lam_h, r.lam), (cot_h, r.cot), (gain_h, r.gain)]
-        )
+        for i, (src, dst) in enumerate([(q_h, r.q), (lam_h, r.lam), (cot_h, r.cot), (gain_h, r.gain)])
     ]
-    for copy in ins[:2]:
-        copy.start()
 
     barrier = pltpu.get_barrier_semaphore()
 
@@ -223,18 +241,15 @@
                 device_id_type=MESH,
             )
 
-    ins[0].wait()
-    ins[1].wait()
-    for copy in ins[2:]:
-        copy.start()
     for i, d in enumerate(Y_TURNS + (0,)):
         h = ahead(y, d, NY)
         lanes = head_lanes(h)
-        acc = jnp.zeros((D, D), F32)
-        for c in range(NC):
-            r.prefix[h * NC + c] = acc.astype(BF16)
-            rows = slice(c * C, (c + 1) * C)
-            acc = acc + dot_tn(r.k[rows, lanes], r.v[rows, lanes])
+        for copy in kv[d]:
+            copy.wait()
+        if i == 0:
+            for copy in ins:
+                copy.start()
+        acc = dot_tn(r.k[:, lanes], r.v[:, lanes])
         if d == 0:
             r.h_y[y] = acc
         else:
@@ -272,13 +287,21 @@
                 )
         return carry
 
-    ins[2].wait()
+    ins[0].wait()
     pass_on(0, 1)
+    for h in range(HL):
+        lanes = head_lanes(h)
+        acc = jnp.zeros((D, D), F32)
+        for c in range(NC):
+            r.prefix[h * NC + c] = acc.astype(BF16)
+            if c < NC - 1:
+                rows = slice(c * C, (c + 1) * C)
+                acc = acc + dot_tn(r.k[rows, lanes], r.v[rows, lanes])
     lax.fori_loop(0, 2, local_step, 0)
     pl.semaphore_wait(r.ring.at[0], 2)
     pass_on(1, 2)
     lax.fori_loop(2, NC, local_step, 0)
-    ins[3].wait()
+    ins[1].wait()
     for level in range(6):
         r.lam_rows[level * HL : (level + 1) * HL, :] = r.lam[level]
     r.lam_rows[6 * HL :, :] = jnp.zeros((D - 6 * HL, T), F32)
@@ -293,17 +316,17 @@
     r.a_own[...] = low
     r.t_own[...] = low + (r.h_y[2] + r.h_y[3])
     pl.semaphore_wait(r.ring.at[1], 2)
-    for d in Z_TURNS:
-        o = ahead(z, d, NZ)
+    for d in Q_TURNS:
+        o = ahead(zi, d, NQ)
         send(
             True,
             r.t_own.at[sub_rows(o), :],
-            r.t_z.at[z],
+            r.t_z.at[zi],
             r.s_tz.at[d],
             r.r_tz.at[d],
-            at_z(o),
-        )
-    r.t_z[z] = r.t_own[sub_rows(z), :]
+            at_quad(o),
+        )
+    r.t_z[zi] = r.t_own[sub_rows(zi), :]
     up, down = ahead(z, 1, NZ), behind(z, 1, NZ)
     send(z_even, r.t_own, r.b_own.at[0], r.s_t0.at[0], r.r_t0.at[0], at_z(up))
     for o in (1, 3):
@@ -352,33 +375,34 @@
     receive(zbit[0], r.b_own.at[0], r.s_t0.at[0], r.r_t0.at[0], at_z(down))
     share_bucket(0)
 
-    for d in Z_TURNS:
-        o = behind(z, d, NZ)
-        receive(True, r.t_z.at[o], r.s_tz.at[d], r.r_tz.at[d], at_z(o))
+    for d in Q_TURNS:
+        o = behind(zi, d, NQ)
+        receive(True, r.t_z.at[o], r.s_tz.at[d], r.r_tz.at[d], at_quad(o))
     low = r.t_z[0] + r.t_z[1]
-    r.pair_z[0] = low
-    r.pair_z[1] = r.t_z[4] + r.t_z[5]
+    r.pair_z[...] = low
     r.quad_z[...] = low + (r.t_z[2] + r.t_z[3])
-    for b in (2, 1):
-        for d in Z_TURNS:
-            o = ahead(z, d, NZ)
-            src = (None, r.pair_z.at[o // 4], r.quad_z)[b]
-            send(
-                bit(o, b),
-                src,
-                r.b_own.at[b, sub_rows(z), :],
-                r.s_bz.at[b, d],
-                r.r_bz.at[b, d],
-                at_z(o),
-            )
+    for k in range(NQ):
+        send(
+            quad == 0,
+            r.quad_z,
+            r.b_own.at[2, sub_rows(zi), :],
+            r.s_bz.at[2, k],
+            r.r_bz.at[2, zi],
+            at_z(NQ + ahead(zi, k, NQ)),
+        )
+    for o in (2, 3):
+        send(
+            zi != o,
+            r.pair_z,
+            r.b_own.at[1, sub_rows(zi), :],
+            r.s_bz.at[1, o],
+            r.r_bz.at[1, zi],
+            at_quad(o),
+        )
 
     @pl.when(zbit[1])
     def _():
-        r.b_own[1, sub_rows(z), :] = r.pair_z[z // 4]
-
-    @pl.when(zbit[2])
-    def _():
-        r.b_own[2, sub_rows(z), :] = r.quad_z[...]
+        r.b_own[1, sub_rows(zi), :] = r.pair_z[...]
 
     def take_bucket(b, there):
         @pl.when(there)
@@ -417,14 +441,13 @@
         return carry
 
     for b in (2, 1):
-        for d in Z_TURNS:
-            o = behind(z, d, NZ)
+        for o in range(NQ):
             receive(
-                zbit[b],
+                zbit[2] if b == 2 else zbit[1] & (zi != o),
                 r.b_own.at[b, sub_rows(o), :],
-                r.s_bz.at[b, d],
-                r.r_bz.at[b, d],
-                at_z(o),
+                r.s_bz.at[b, o],
+                r.r_bz.at[b, o],
+                at_quad(o),
             )
         share_bucket(b)
 
@@ -439,8 +462,8 @@
             )
         take_bucket(b, there)
     receive_bucket(0)
-    ins[4].wait()
-    ins[5].wait()
+    ins[2].wait()
+    ins[3].wait()
 
     lax.fori_loop(0, NC, first_step, 0)
 
@@ -472,7 +495,7 @@
         r.stat_own[1:2, rows] = dot_nt(ones, jnp.concatenate(inners, axis=1))[0:1]
         return carry
 
-    lax.fori_loop(0, NC, out_step, 0)
+    lax.fori_loop(0, NC, out_step, 0, unroll=True)
 
     for d in HEAD_TURNS:
         o = ahead(head, d, NH)
@@ -496,6 +519,9 @@
             r.reads[h, rows, 3 * D :] = dot_nn(r.q[rows, head_lanes(h)], r.bcat[h, :, 3 * D :])
         return carry
 
+    later, sent[:] = sent[-len(HEAD_TURNS) :], sent[: -len(HEAD_TURNS)]
+    drain()
+    sent += later
     lax.fori_loop(0, NC, high_reads_step, 0)
     lax.fori_loop(0, NC, kept_step, 0)
 
@@ -648,7 +674,6 @@
             r.ds[h * NC + c] = dot_nn(r.q_t[h, :, rows], ec)
         return carry
 
-    lax.fori_loop(0, NC, query_step, 0)
     lax.fori_loop(0, 2, key_step, 0)
 
     def sum_over_y(level):
@@ -660,17 +685,17 @@
         @pl.when(zbit[b])
         def _(b=b):
             r.u_own[b] = sum_over_y(b + 2)
-            r.u_z[b, z] = r.u_own[b, sub_rows(z), :]
-
-        for d in Z_TURNS:
-            o = ahead(z, d, NZ)
+            r.u_z[b, zi] = r.u_own[b, sub_rows(zi), :]
+
+        for d in Q_TURNS:
+            o = ahead(zi, d, NQ)
             send(
                 zbit[b],
                 r.u_own.at[b, sub_rows(o), :],
-                r.u_z.at[b, z],
+                r.u_z.at[b, zi],
                 r.s_uz.at[b, d],
                 r.r_uz.at[b, d],
-                at_z(o),
+                at_quad(o),
             )
     for d in Y_TURNS:
         o = ahead(y, d, NY)
@@ -684,7 +709,7 @@
         )
     r.gg_y[y, 0:1, :] = r.gg_own[0:1, :]
 
-    lax.fori_loop(2, NC, key_step, 0)
+    lax.fori_loop(0, 2, query_step, 0)
 
     receive_grad(2, lambda o: zbit[0])
 
@@ -693,40 +718,46 @@
         r.u_own[0] = sum_over_y(2)
 
     send(zbit[0], r.u_own.at[0], r.u0_in, r.s_u0.at[0], r.r_u0.at[0], at_z(down))
-    lax.fori_loop(0, 1, level_step, 0)
+    lax.fori_loop(2, NC, query_step, 0)
 
     for b in (2, 1):
-        for d in Z_TURNS:
-            o = behind(z, d, NZ)
-            receive(bit(o, b), r.u_z.at[b, o], r.s_uz.at[b, d], r.r_uz.at[b, d], at_z(o))
-    quad = (r.u_z[2, 4] + r.u_z[2, 5]) + (r.u_z[2, 6] + r.u_z[2, 7])
-    pair_low = r.u_z[1, 2] + r.u_z[1, 3]
-    pair_high = r.u_z[1, 6] + r.u_z[1, 7]
-    low = pair_low + quad
-    r.g_z[0] = low
-    r.g_z[1] = low
-    r.g_z[2] = quad
-    r.g_z[3] = quad
-    r.g_z[4] = pair_high
-    r.g_z[5] = pair_high
-    for d in Z_TURNS:
-        o = ahead(z, d, NZ)
+        for d in Q_TURNS:
+            o = behind(zi, d, NQ)
+            receive(
+                zbit[2] if b == 2 else bit(o, 1),
+                r.u_z.at[b, o],
+                r.s_uz.at[b, d],
+                r.r_uz.at[b, d],
+                at_quad(o),
+            )
+
+    @pl.when(zbit[2])
+    def _():
+        r.g_z[1] = (r.u_z[2, 0] + r.u_z[2, 1]) + (r.u_z[2, 2] + r.u_z[2, 3])
+
+    for k in range(NQ):
         send(
-            o < 6,
-            r.g_z.at[o],
-            r.g_own.at[sub_rows(z), :],
-            r.s_gz.at[d],
-            r.r_gz.at[d],
-            at_z(o),
-        )
-
-    @pl.when(z < 6)
+            zbit[2],
+            r.g_z.at[1],
+            r.g_in.at[1, sub_rows(zi), :],
+            r.s_gz.at[1, k],
+            r.r_gz.at[1, zi],
+            at_z(ahead(zi, k, NQ)),
+        )
+    r.g_z[0] = r.u_z[1, 2] + r.u_z[1, 3]
+    for o in (0, 1):
+        send(
+            zi != o,
+            r.g_z.at[0],
+            r.g_in.at[0, sub_rows(zi), :],
+            r.s_gz.at[0, o],
+            r.r_gz.at[0, zi],
+            at_quad(o),
+        )
+
+    @pl.when(zi < 2)
     def _():
-        r.g_own[sub_rows(z), :] = r.g_z[z]
-
-    @pl.when(z >= 6)
-    def _():
-        r.g_own[...] = jnp.zeros((D, D), F32)
+        r.g_in[0, sub_rows(zi), :] = r.g_z[0]
 
     for d in Y_TURNS:
         o = behind(y, d, NY)
@@ -746,14 +777,37 @@
         )
     r.gg_z[z, 0:1, :] = r.gg_mid[0:1, :]
 
-    lax.fori_loop(1, NC, level_step, 0)
+    lax.fori_loop(2, NC, key_step, 0)
+    lax.fori_loop(0, 2, level_step, 0)
 
     for b in range(2):
         receive_grad(b, lambda o: bit(o, b))
     receive(z_even, r.u0_in, r.s_u0.at[0], r.r_u0.at[0], at_z(up))
-    for d in Z_TURNS:
-        o = behind(z, d, NZ)
-        receive(z < 6, r.g_own.at[sub_rows(o), :], r.s_gz.at[d], r.r_gz.at[d], at_z(o))
+    for o in range(NQ):
+        receive(
+            (zi < 2) & (zi != o),
+            r.g_in.at[0, sub_rows(o), :],
+            r.s_gz.at[0, o],
+            r.r_gz.at[0, o],
+            at_quad(o),
+        )
+    for o in range(NQ):
+        receive(
+            quad == 0,
+            r.g_in.at[1, sub_rows(o), :],
+            r.s_gz.at[1, o],
+            r.r_gz.at[1, o],
+            at_z(o),
+        )
+    r.g_own[...] = jnp.zeros((D, D), F32)
+
+    @pl.when(zi < 2)
+    def _():
+        r.g_own[...] += r.g_in[0]
+
+    @pl.when(quad == 0)
+    def _():
+        r.g_own[...] += r.g_in[1]
 
     @pl.when(z_even)
     def _():
@@ -769,8 +823,20 @@
         o = ahead(y, d, NY)
         send(True, r.dh_own.at[o], r.dh.at[y], r.s_dh.at[d], r.r_dh.at[d], at_y(o))
     r.dh[y] = r.dh_own[y]
-
-    for d in (0,) + Y_TURNS:
+    lax.fori_loop(2, NC, level_step, 0)
+    later, sent[:] = sent[-len(Y_TURNS) :], sent[: -len(Y_TURNS)]
+    drain()
+    sent += later
+    for d in Z_TURNS:
+        o = behind(z, d, NZ)
+        receive(True, r.gg_z.at[o, pl.ds(0, 1), :], r.s_ggz.at[d], r.r_ggz.at[d], at_z(o))
+    total = r.gg_z[0, 0:1, :]
+    for o in range(1, NZ):
+        total = total + r.gg_z[o, 0:1, :]
+    gg_o[...] = total
+
+
+    for d in (0,) + Y_ARRIVALS:
         h = behind(y, d, NY)
         lanes = head_lanes(h)
         if d:
@@ -787,16 +853,7 @@
             )
             acc = acc + r.ds[h * NC + c]
 
-    for d in Z_TURNS:
-        o = behind(z, d, NZ)
-        receive(True, r.gg_z.at[o, pl.ds(0, 1), :], r.s_ggz.at[d], r.r_ggz.at[d], at_z(o))
-    total = r.gg_z[0, 0:1, :]
-    for o in range(1, NZ):
-        total = total + r.gg_z[o, 0:1, :]
-    gg_o[...] = total
-
-    for cond, make in sent:
-        when(cond, lambda make=make: make().wait_send())
+    drain()
 
 
 def store_kernel(*refs):

time: 67.1 us -> 64.9 us (0.967)
  Pallas kernels: 66.2 us -> 63.6 us
    pallas_call x1, Pallas kernels: 64.1 us -> 61.5 us  [body(): pl.pallas_call(kernel, out_shape=tuple((pltpu.VMEM(*shape) for shape in s...]
where the time goes in v4:
time: 64.9 us; the launch traced here: 64.4 us
  Pallas kernels  63.6 us (98%)
  between operations  0.8 us (1%)
    pallas_call x1, Pallas kernels, body(): pl.pallas_call(kernel, out_shape=tuple((pltpu.VMEM(*shape) for shape in s...  61.5 us
    pallas_call x1, Pallas kernels, body(): pl.pallas_call(store_kernel, out_shape=tuple((jax.ShapeDtypeStruct(*shape...  2.08 us

profile of v4, /device:TPU:6, one launch (start us, length us, event | category | flops | bytes accessed | tf_op | source)
XLA Modules:
  0.0 64.4 jit_solution(15633929046488522686)
XLA Ops:
  0.6 61.5 %shard_map.109 = (bf16[1024,512]{1,0:T(8,128)(2,1)S(1)}, bf16[1024,512]{1,0:T(8,128)(2,1)S(1)}, bf16[1024,512]{1,0:T(8,128)(2,1)S(1)}, bf16[1024,512]{1,0:T(8,12...) custom-call(bf16[1024,512]{1,0:T(8,128)(2,1)} %q_h.1, bf16[1024,512]{1,0:T(8,128)(2,1)} %k_h.1, ...), custom_call_target="tpu_custom_call" | custom-call | tf_op jit(solution)/shard_map/pallas_call | solution.py:872
  62.1 2.1 %shard_map.110 = (bf16[1024,512]{1,0:T(8,128)(2,1)}, bf16[1024,512]{1,0:T(8,128)(2,1)}, bf16[1024,512]{1,0:T(8,128)(2,1)}, bf16[1024,512]{1,0:T(8,128)(2,1)}, f32[6,4,1024]{2,1,0:T(4,128)}, /*index=5*/f32[1,512]{1,0:T(1,128)}) custom-call(bf16[1024,512]{1,0:T(8,128)(2,1)S(1)} %get-tuple-element.18.refs_0_, bf16[1024,512]{1,0:T(8,128)(2,1)S(1)} %get-tuple-element.19.refs_1_, ...), custom_call_target="tpu_custom_call" | custom-call | tf_op jit(solution)/shard_map/pallas_call | solution.py:882
